TPU v7x, 512 devices: a whole 4x8x8 slice. The times are simulated.
512 devices in a mesh: grp: 16 (over z, core), ep: 32 (over x, y).
Axes of the slice: x: 4, y: 8, z: 8, core: 2. Of those that a mesh axis runs over, the one named last changes fastest.
Arguments:
- q_raw: bfloat16 [8192, 4096], P(('grp', 'ep')), may hold values from -6 to 6
- k_raw: bfloat16 [8192, 512], P(('grp', 'ep')), may hold values from -6 to 6
- v_raw: bfloat16 [8192, 512], P(('grp', 'ep')), may hold values from -6 to 6
- q_gain: float32 [128], replicated, may hold values from 0.5 to 1.5
- k_gain: float32 [128], replicated, may hold values from 0.5 to 1.5
- caches: bfloat16 [16, 1024, 2, 2, 512], P('grp', 'ep'), may hold values from -4 to 4
- lengths: int32 [16, 32], P('grp', 'ep'), may hold values from 1 to 16, 448 in all within a row
- cont_owner: int32 [16, 32], P('grp', 'ep'), may hold values from 0 to 31, as said below
- out_weight: bfloat16 [4096, 2048], P(None, 'grp'), may hold values from -1 to 1
- residual: bfloat16 [8192, 2048], P(('grp', 'ep')), may hold values from -24 to 24
- moe_gain: float32 [2048], replicated, may hold values from 0.1 to 1.9
- routes: int32 [8192, 8], P(('grp', 'ep')), may hold values from 0 to 127, all different within a row; in each aligned block of 16 rows (0 to 15, 16 to 31, ...) at most 2 rows name the same one
- gate_weights: float32 [8192, 8], P(('grp', 'ep')), may hold values from 0.05 to 0.3
- w_in: bfloat16 [2, 2048, 98304], P(None, None, ('grp', 'ep')), may hold values from -0.125 to 0.125
- w_down: bfloat16 [98304, 2048], P(('grp', 'ep')), may hold values from -0.21875 to 0.21875
Outputs:
- mixed: bfloat16 [8192, 2048], P(('grp', 'ep'))
Inputs may be any that keep to these rules, and one draw needn't show every extreme that they name: `routes`: in the rows of one device (aligned blocks of 16 rows) no expert is named by more than 2 rows, a bound that some block reaches. The 32 lengths of a group sum to 448 and the longest is 16. `cont_owner`: entry [g, p] names a device of group g; for some requests it is p itself.
All inputs are finite; a program needn't handle non-finite values.
Results may differ from a plain program's by a relative error of at most 0.0065.
The roundings to bfloat16 on the way count: a program that leaves them out, or rounds other values in their place, can miss the bound.
Values may be sent and summed in bfloat16 or wider, within the bound.
A program may use at most 64 MiB of HBM per device.

v0:
```python
import math

import jax
import jax.numpy as jnp
from jax import lax
from jax.sharding import PartitionSpec as P

theta_base = 1000000.0
eps_norm = 1e-06


def normed(values, scales):
    return values * lax.rsqrt(jnp.mean(values * values, axis=-1, keepdims=True) + eps_norm) * scales


def rotate(values, position):
    head_width = values.shape[-1]
    half_width = head_width // 2
    inv_freq = jnp.power(theta_base, -2.0 * jnp.arange(half_width, dtype=jnp.float32) / head_width)
    angles = position[:, None] * inv_freq[None, :]
    cosine = jnp.cos(angles)[:, None, :]
    sine_part = jnp.sin(angles)[:, None, :]
    first_half = values[..., :half_width]
    second_half = values[..., half_width:]
    return jnp.concatenate(
        [
            first_half * cosine - second_half * sine_part,
            second_half * cosine + first_half * sine_part,
        ],
        axis=-1,
    )


def per_device(
    q_raw,
    k_raw,
    v_raw,
    q_gain,
    k_gain,
    caches,
    lengths,
    cont_owner,
    out_weight,
    residual,
    moe_gain,
    routes,
    gate_weights,
    w_in,
    w_down,
):
    n_groups = lax.axis_size("grp")
    n_columns = lax.axis_size("ep")
    tok_count, model_width = residual.shape
    head_dim = q_gain.shape[0]
    kv_heads = k_raw.shape[1] // head_dim
    q_heads = q_raw.shape[1] // head_dim
    group_size = q_heads // kv_heads
    cache_rows = caches.shape[1]
    top_count = routes.shape[1]
    pieces = 4
    expert_count = n_groups * n_columns // pieces
    capacity = max(2, tok_count * top_count // expert_count)
    scaling = 1.0 / math.sqrt(head_dim)
    seq_len = lengths[0, 0]
    owner_col = cont_owner[0, 0]
    token_idx = jnp.arange(tok_count, dtype=jnp.int32)
    live_rows = token_idx < seq_len
    position = (cache_rows * n_columns + cache_rows + token_idx).astype(jnp.float32)
    queries = normed(q_raw.astype(jnp.float32).reshape(tok_count, q_heads, head_dim), q_gain)
    queries = (
        rotate(queries, position)
        .astype(jnp.bfloat16)
        .reshape(tok_count, kv_heads, group_size, head_dim)
    )
    own_keys = normed(k_raw.astype(jnp.float32).reshape(tok_count, kv_heads, head_dim), k_gain)
    own_keys = rotate(own_keys, position).astype(jnp.bfloat16)
    own_values = v_raw.reshape(tok_count, kv_heads, head_dim)

    def weigh_keys(key_rows, key_mask):
        scores = (
            jnp.einsum("tkgd,nkd->tkgn", queries, key_rows, preferred_element_type=jnp.float32)
            * scaling
        )
        return jnp.where(key_mask, jnp.exp(scores), 0.0)

    def accumulate(running, weights, value_rows):
        numerator, denominator = running
        numerator = numerator + jnp.einsum(
            "tkgn,nkd->tkgd",
            weights.astype(jnp.bfloat16),
            value_rows,
            preferred_element_type=jnp.float32,
        )
        denominator = denominator + jnp.sum(weights, axis=-1)
        return (numerator, denominator)

    start_state = (
        jnp.zeros((tok_count, kv_heads, group_size, head_dim), jnp.float32),
        jnp.zeros((tok_count, kv_heads, group_size), jnp.float32),
    )
    running = start_state
    kv_block = lax.all_gather(caches[0], "ep", axis=0, tiled=True)
    row_count = kv_block.shape[0]
    source = jnp.arange(row_count, dtype=jnp.int32) // cache_rows
    pre_keys = kv_block[:, 0, 0].reshape(row_count, kv_heads, head_dim)
    pre_values = kv_block[:, 0, 1].reshape(row_count, kv_heads, head_dim)
    cont_keys = kv_block[:, 1, 0].reshape(row_count, kv_heads, head_dim)
    cont_values = kv_block[:, 1, 1].reshape(row_count, kv_heads, head_dim)
    everywhere = jnp.ones((row_count,), dtype=bool)
    running = accumulate(running, weigh_keys(pre_keys, everywhere), pre_values)
    running = accumulate(running, weigh_keys(cont_keys, source == owner_col), cont_values)
    causal_mask = (token_idx[None, :] <= token_idx[:, None]) & (token_idx[None, :] < seq_len)
    numerator, denominator = accumulate(
        running, weigh_keys(own_keys, causal_mask[:, None, None, :]), own_values
    )
    attended = jnp.where(live_rows[:, None, None, None], numerator / denominator[..., None], 0.0)
    attended = attended.astype(jnp.bfloat16).reshape(tok_count, q_heads * head_dim)
    projected = jnp.dot(
        lax.all_gather(attended, "grp", axis=0, tiled=True),
        out_weight,
        preferred_element_type=jnp.float32,
    ).astype(jnp.bfloat16)
    attn_proj = lax.all_to_all(projected, "grp", split_axis=0, concat_axis=1, tiled=True)
    hidden_state = (residual.astype(jnp.float32) + attn_proj.astype(jnp.float32)).astype(
        jnp.bfloat16
    )
    moe_in = normed(hidden_state.astype(jnp.float32), moe_gain).astype(jnp.bfloat16)
    flat_route = jnp.where(live_rows[:, None], routes, -1).reshape(-1)
    assign_idx = jnp.arange(flat_route.shape[0], dtype=jnp.int32)
    matches = (flat_route[:, None] == flat_route[None, :]) & (
        assign_idx[None, :] < assign_idx[:, None]
    )
    slot_rank = jnp.sum(matches.astype(jnp.int32), axis=1)
    expert_hot = flat_route[:, None] == jnp.arange(expert_count, dtype=jnp.int32)[None, :]
    slot_hot = slot_rank[:, None] == jnp.arange(capacity, dtype=jnp.int32)[None, :]
    placed = (
        (expert_hot[:, :, None] & slot_hot[:, None, :])
        .astype(jnp.float32)
        .reshape(tok_count, top_count, expert_count, capacity)
    )
    chosen = jnp.sum(placed, axis=1).astype(jnp.bfloat16)
    weighted = jnp.sum(gate_weights[:, :, None, None] * placed, axis=1)
    dispatch = jnp.einsum("tec,tf->ecf", chosen, moe_in, preferred_element_type=jnp.float32).astype(
        jnp.bfloat16
    )
    outgoing = jnp.broadcast_to(dispatch[:, None], (expert_count, pieces, capacity, model_width))
    outgoing = outgoing.reshape(n_groups, n_columns, capacity, model_width)
    received = lax.all_to_all(
        lax.all_to_all(outgoing, "grp", split_axis=0, concat_axis=0, tiled=True),
        "ep",
        split_axis=1,
        concat_axis=1,
        tiled=True,
    )
    rows_in = received.reshape(-1, model_width)
    gate_act = jnp.dot(rows_in, w_in[0], preferred_element_type=jnp.float32)
    up_act = jnp.dot(rows_in, w_in[1], preferred_element_type=jnp.float32)
    inner_act = (jax.nn.silu(gate_act) * up_act).astype(jnp.bfloat16)
    partial_out = jnp.dot(inner_act, w_down, preferred_element_type=jnp.float32).astype(
        jnp.bfloat16
    )
    partial_out = partial_out.reshape(n_groups, n_columns, capacity, model_width)
    returned = lax.all_to_all(
        lax.all_to_all(partial_out, "grp", split_axis=0, concat_axis=0, tiled=True),
        "ep",
        split_axis=1,
        concat_axis=1,
        tiled=True,
    )
    summed = jnp.sum(
        returned.reshape(expert_count, pieces, capacity, model_width).astype(jnp.float32), axis=1
    )
    expert_out = summed.astype(jnp.bfloat16).astype(jnp.float32)
    moe_out = jnp.einsum("tec,ecf->tf", weighted, expert_out, precision=lax.Precision.HIGHEST)
    mixed = jnp.where(live_rows[:, None], hidden_state.astype(jnp.float32) + moe_out, 0.0)
    return mixed.astype(jnp.bfloat16)


def solution(mesh):
    in_specs = (
        P(("grp", "ep"), None),
        P(("grp", "ep"), None),
        P(("grp", "ep"), None),
        P(),
        P(),
        P("grp", "ep", None, None, None),
        P("grp", "ep"),
        P("grp", "ep"),
        P(None, "grp"),
        P(("grp", "ep"), None),
        P(),
        P(("grp", "ep"), None),
        P(("grp", "ep"), None),
        P(None, None, ("grp", "ep")),
        P(("grp", "ep"), None),
    )
    out_specs = P(("grp", "ep"), None)
    return jax.shard_map(
        per_device, mesh=mesh, in_specs=in_specs, out_specs=out_specs, check_vma=False
    )
```

profile of v0, /device:TPU:1, one launch (start us, length us, event | category | flops | bytes accessed | tf_op | source)
XLA Modules:
  0.0 654.9 jit_solution(9818329224442656791)
XLA Ops:
  6.5 0.7 all-gather.6.cloned.1.call-update
  8.6 0.7 reshape.219
  9.3 0.7 reshape.228
  10.2 0.9 convert_bitcast_fusion
  11.5 0.8 multiply_multiply_fusion
  13.6 85.9 %all-gather.6.cloned.1.call-done = bf16[1,1024,2,2,512]{4,3,2,0,1:T(2,128)(2,1)} async-done(((bf16[1,32,2,2,512]{4,3,2,0,1:T(2,128)(2,1)}), bf16[1,1024,2,2,512]{4,3,2,0,1:T(2,128)(2,1)}) %all-gather.6.cloned.1.call-update) | async-done | bytes 4194320 | tf_op jit(solution)/shard_map/all_gather | solution.py:102
  99.5 11.2 %copy.143 = bf16[1,1024,2,2,512]{1,4,3,2,0:T(8,128)(2,1)} copy(bf16[1,1024,2,2,512]{4,3,2,0,1:T(2,128)(2,1)} %all-gather.6.cloned.1.call-done) | data formatting | bytes 8388608 | tf_op jit(solution)/shard_map/all_gather | solution.py:102
  110.7 2.6 fusion.65
  113.3 0.6 bitcast_reduce_fusion.1
  113.9 0.7 bitcast_reduce_fusion
  115.1 0.5 convolution_add_fusion.1
  115.9 0.7 copy.213
  117.3 43.5 %all-gather.4.cloned.1.call-done = bf16[256,4096]{1,0:T(8,128)(2,1)} async-done(((bf16[16,4096]{1,0:T(8,128)(2,1)}), bf16[256,4096]{1,0:T(8,128)(2,1)}) %all-gather.4.cloned.1.call-update) | async-done | bytes 2097168 | tf_op jit(solution)/shard_map/all_gather | solution.py:119
  160.8 2.9 convolution_convert_fusion.2
  163.7 4.4 all-to-all-start
  168.3 7.6 %all-to-all-done = bf16[16,16,128]{2,1,0:T(8,128)(2,1)S(1)} async-done(((bf16[16,16,128]{2,1,0:T(8,128)(2,1)}), bf16[16,16,128]{2,1,0:T(8,128)(2,1)S(1)}, u32[]{:S(2)}, u32[]{:S(2)}) %all-to-all-start) | async-done | bytes 65568 | tf_op jit(solution)/shard_map/all_to_all | solution.py:123
  176.6 1.1 copy.160
  177.7 4.6 broadcast_in_dim.65
  182.2 99.6 %all_to_all.33 = bf16[16,32,2,2048]{3,2,1,0:T(2,128)(2,1)S(1)} all-to-all(bf16[16,32,2,2048]{3,2,1,0:T(2,128)(2,1)} %bitcast.114), channel_id=1, replica_groups=mesh['grp'=16,'ep'=32] {'grp'}, dimensions={0} | all-to-all | bytes 8388608 | tf_op jit(solution)/shard_map/all_to_all | solution.py:149
  281.9 6.5 copy.161
  288.3 104.9 %all_to_all.34 = bf16[16,32,2,2048]{3,2,0,1:T(2,128)(2,1)S(1)} all-to-all(bf16[16,32,2,2048]{3,2,0,1:T(2,128)(2,1)} %copy.161), channel_id=1, replica_groups=mesh['grp'=16,'ep'=32] {'ep'}, dimensions={1} | all-to-all | bytes 8388608 | tf_op jit(solution)/shard_map/all_to_all | solution.py:148
  393.2 6.0 copy.162
  399.2 7.2 %reshape.222 = bf16[1024,2048]{1,0:T(8,128)(2,1)} reshape(bf16[16,32,2,2048]{3,2,1,0:T(2,128)(2,1)} %copy.162) | data formatting | bytes 8388608 | tf_op jit(solution)/shard_map/reshape | solution.py:155
  406.5 4.0 fusion.19
  410.5 7.1 %convolution_convert_fusion = bf16[1024,2048]{1,0:T(8,128)(2,1)} fusion(bf16[192,2048]{1,0:T(8,128)(2,1)S(1)} %copy-done.8, bf16[1024,2048]{1,0:T(8,128)(2,1)} %reshape.222, bf16[2,2048,192]{1,2,0:T(8,128)(2,1)} %param.28, f32[1024,192]{0,1:T(8,128)S(1)} %fusion.19), kind=kOutput, calls=%fused_computation | convolution fusion | flops 1613889536 | bytes 10747904 | tf_op jit(solution)/shard_map/dot_general | solution.py:159
  417.5 7.6 %reshape.223 = bf16[16,32,2,2048]{3,2,1,0:T(2,128)(2,1)} reshape(bf16[1024,2048]{1,0:T(8,128)(2,1)} %convolution_convert_fusion) | data formatting | bytes 8388608 | tf_op jit(solution)/shard_map/reshape | solution.py:162
  425.2 99.7 %all_to_all.35 = bf16[16,32,2,2048]{3,2,1,0:T(2,128)(2,1)S(1)} all-to-all(bf16[16,32,2,2048]{3,2,1,0:T(2,128)(2,1)} %reshape.223), channel_id=1, replica_groups=mesh['grp'=16,'ep'=32] {'grp'}, dimensions={0} | all-to-all | bytes 8388608 | tf_op jit(solution)/shard_map/all_to_all | solution.py:164
  524.8 6.5 copy.163
  531.3 100.8 %all_to_all.36 = bf16[16,32,2,2048]{3,2,0,1:T(2,128)(2,1)S(1)} all-to-all(bf16[16,32,2,2048]{3,2,0,1:T(2,128)(2,1)} %copy.163), channel_id=1, replica_groups=mesh['grp'=16,'ep'=32] {'ep'}, dimensions={1} | all-to-all | bytes 8388608 | tf_op jit(solution)/shard_map/all_to_all | solution.py:163
  632.1 6.0 copy.164
  638.1 8.3 %reduce_sum.102 = bf16[128,2,2048]{2,1,0:T(2,128)(2,1)S(1)} reduce(bf16[128,4,2,2048]{3,2,1,0:T(2,128)(2,1)} %bitcast.116, bf16[]{:T(256)} %constant.52.clone.1), dimensions={1}, to_apply=%region_9.10 | reduce | flops 1572864 | bytes 5242882 | tf_op jit(solution)/shard_map/reduce_sum | solution.py:170
  646.4 1.6 fusion.2
  (56 shorter events, 3.9 us)
Async XLA Ops:
  6.5 154.3 %copy-start = (bf16[4096,128]{1,0:T(8,128)(2,1)S(1)}, bf16[4096,128]{1,0:T(8,128)(2,1)}, u32[]{:S(2)}) copy-start(bf16[4096,128]{1,0:T(8,128)(2,1)} %param.23) | copy-start | bytes 3145732
  6.5 6.2 copy-start.3
  6.5 6.2 copy-start.7
  6.5 93.0 %all-gather.6.cloned.1.call-start = ((), (), s32[]{:S(2)}) async-start(), calls=%async_computation.6 | async-start | bytes 4325376 | tf_op jit(solution)/shard_map/all_gather | solution.py:102
  7.3 153.6 %all-gather.4.cloned.1.call-start = ((), (), s32[]{:S(2)}) async-start(), calls=%async_computation.5 | async-start | bytes 2228224 | tf_op jit(solution)/shard_map/all_gather | solution.py:119
  115.1 1.5 copy-start.6
  115.1 2.0 copy-start.5
  115.8 60.1 %copy-start.2 = (bf16[16,2048]{1,0:T(8,128)(2,1)S(1)}, bf16[16,2048]{1,0:T(8,128)(2,1)}, u32[]{:S(2)}) copy-start(bf16[16,2048]{1,0:T(8,128)(2,1)} %param.24) | copy-start | bytes 196612
  115.9 60.2 %copy-start.4 = (f32[2048]{0:T(1024)S(1)}, f32[2048]{0:T(1024)}, u32[]{:S(2)}) copy-start(f32[2048]{0:T(1024)} %param.25) | copy-start | bytes 24580
  163.7 12.2 %all-to-all-start = ((bf16[16,16,128]{2,1,0:T(8,128)(2,1)}), bf16[16,16,128]{2,1,0:T(8,128)(2,1)S(1)}, u32[]{:S(2)}, u32[]{:S(2)}) async-start(bf16[16,16,128]{2,1,0:T(8,128)(2,1)} %bitcast.21), calls=%async_computation | async-start | bytes 131072 | tf_op jit(solution)/shard_map/all_to_all | solution.py:123
  406.5 4.0 copy-start.8
  638.1 10.0 %copy-start.1 = (bf16[4096,128]{1,0:T(8,128)(2,1)S(1)}, bf16[4096,128]{1,0:T(8,128)(2,1)}, u32[]{:S(2)}) copy-start(bf16[4096,128]{1,0:T(8,128)(2,1)} %param.23) | copy-start | bytes 3145732
Sparse Core Ops, SparseCore 0:
  10.5 88.9 all-gather.5
  116.8 44.0 all-gather.3
where the time goes:
time: 656 us; the launch traced here: 655 us
  blocking collectives  405 us (62%)
  waiting for transfers between devices  138 us (21%)
  local copies, waits for them, and re-layouts  62.1 us (9%)
  matrix products  19 us (3%)
  between operations  15 us (2%)
  other arithmetic  11.5 us (2%)
    all_to_all x1, blocking collectives, per_device(): lax.all_to_all(lax.all_to_all(outgoing, 'grp', split_axis=0, concat_axis=...  105 us
    all_to_all x1, blocking collectives, per_device(): lax.all_to_all(lax.all_to_all(partial_out, 'grp', split_axis=0, concat_ax...  101 us
    all_to_all x1, blocking collectives, per_device(): lax.all_to_all(partial_out, 'grp', split_axis=0, concat_axis=0, tiled=True)  99.7 us
    all_to_all x1, blocking collectives, per_device(): lax.all_to_all(outgoing, 'grp', split_axis=0, concat_axis=0, tiled=True)  99.6 us
    all_gather x1, waiting for transfers between devices, per_device(): kv_block = lax.all_gather(caches[0], 'ep', axis=0, tiled=True)  85.9 us
    all_gather x1, waiting for transfers between devices, per_device(): lax.all_gather(attended, 'grp', axis=0, tiled=True)  43.5 us
  transfers between devices with their start and end apart: 3, of which 3 were waited for; matrix products, arithmetic and copies ran while one was open for 1% of the time, Pallas kernels for 0%

commit v1 on v0

v1 whole, which is shorter than its diff:
```python
import functools
import math

import jax
import jax.numpy as jnp
from jax import lax
from jax.experimental import pallas as pl
from jax.experimental.pallas import tpu as pltpu
from jax.sharding import PartitionSpec as P

theta_base = 1000000.0
eps_norm = 1e-06
f32 = jnp.float32
bf16 = jnp.bfloat16


def normed(values, scales):
    return values * lax.rsqrt(jnp.mean(values * values, axis=-1, keepdims=True) + eps_norm) * scales


def rotation_tables(position, head_width):
    half_width = head_width // 2
    inv_freq = jnp.power(theta_base, -2.0 * jnp.arange(half_width, dtype=f32) / head_width)
    angles = position[:, None] * inv_freq[None, :]
    cosine, sine = jnp.cos(angles), jnp.sin(angles)
    return jnp.concatenate([cosine, cosine], -1), jnp.concatenate([-sine, sine], -1)


def attention_body(
    kv_heads, cache_rows, len_ref, own_ref, q_ref, k_ref, v_ref, qg_ref, kg_ref, cos_ref, sin_ref, kv_ref, out_ref
):
    tok_count = q_ref.shape[0]
    hd = qg_ref.shape[1]
    width = kv_heads * hd
    group = q_ref.shape[1] // width
    rows = group * tok_count
    scaling = 1.0 / math.sqrt(hd)
    seq_len = len_ref[0, 0]
    start = pl.multiple_of(own_ref[0, 0] * cache_rows, cache_rows)
    cosine, sine = cos_ref[...], sin_ref[...]

    def prepared(raw, gain):
        values = normed(raw.astype(f32), gain)
        return (values * cosine + pltpu.roll(values, hd // 2, 1) * sine).astype(bf16)

    slot = lax.broadcasted_iota(jnp.int32, (rows, tok_count), 0) % tok_count
    other = lax.broadcasted_iota(jnp.int32, (rows, tok_count), 1)
    causal = (other <= slot) & (other < seq_len)
    live = lax.broadcasted_iota(jnp.int32, (rows, hd), 0) % tok_count < seq_len
    contract = (((1,), (1,)), ((), ()))

    def weighed(queries, keys):
        return jnp.exp(lax.dot_general(queries, keys, contract, preferred_element_type=f32) * scaling)

    for h in range(kv_heads):
        span = pl.ds(h * hd, hd)
        queries = jnp.concatenate(
            [prepared(q_ref[:, pl.ds((h * group + j) * hd, hd)], qg_ref[...]) for j in range(group)], 0
        )
        pre = weighed(queries, kv_ref[:, span])
        cont = weighed(queries, kv_ref[pl.ds(start, cache_rows), pl.ds(2 * width + h * hd, hd)])
        own = jnp.where(causal, weighed(queries, prepared(k_ref[:, span], kg_ref[...])), 0.0)
        numerator = (
            jnp.dot(pre.astype(bf16), kv_ref[:, pl.ds(width + h * hd, hd)], preferred_element_type=f32)
            + jnp.dot(
                cont.astype(bf16),
                kv_ref[pl.ds(start, cache_rows), pl.ds(3 * width + h * hd, hd)],
                preferred_element_type=f32,
            )
            + jnp.dot(own.astype(bf16), v_ref[:, span], preferred_element_type=f32)
        )
        denominator = (
            jnp.sum(pre, 1, keepdims=True) + jnp.sum(cont, 1, keepdims=True) + jnp.sum(own, 1, keepdims=True)
        )
        result = jnp.where(live, numerator / denominator, 0.0).astype(bf16)
        for j in range(group):
            out_ref[:, pl.ds((h * group + j) * hd, hd)] = result[j * tok_count : (j + 1) * tok_count]


def attention(q_raw, k_raw, v_raw, q_gain, k_gain, kv_block, lengths, cont_owner, cache_rows):
    hd = q_gain.shape[0]
    tok_count = q_raw.shape[0]
    position = (kv_block.shape[0] + cache_rows + jnp.arange(tok_count, dtype=jnp.int32)).astype(f32)
    cosine, sine = rotation_tables(position, hd)
    vmem = pl.BlockSpec(memory_space=pltpu.VMEM)
    smem = pl.BlockSpec(memory_space=pltpu.SMEM)
    return pl.pallas_call(
        functools.partial(attention_body, k_raw.shape[1] // hd, cache_rows),
        out_shape=jax.ShapeDtypeStruct(q_raw.shape, bf16),
        in_specs=[smem, smem] + [vmem] * 8,
        out_specs=vmem,
    )(lengths, cont_owner, q_raw, k_raw, v_raw, q_gain[None], k_gain[None], cosine, sine, kv_block)


def per_device(
    q_raw,
    k_raw,
    v_raw,
    q_gain,
    k_gain,
    caches,
    lengths,
    cont_owner,
    out_weight,
    residual,
    moe_gain,
    routes,
    gate_weights,
    w_in,
    w_down,
):
    n_groups = lax.axis_size("grp")
    n_columns = lax.axis_size("ep")
    tok_count, model_width = residual.shape
    cache_rows = caches.shape[1]
    top_count = routes.shape[1]
    pieces = 4
    expert_count = n_groups * n_columns // pieces
    local = expert_count // n_groups
    capacity = 2
    per_source = n_groups * capacity
    live_rows = jnp.arange(tok_count, dtype=jnp.int32) < lengths[0, 0]

    flat_route = jnp.where(live_rows[:, None], routes, -1).reshape(-1)
    assign_idx = jnp.arange(flat_route.shape[0], dtype=jnp.int32)
    matches = (flat_route[:, None] == flat_route[None, :]) & (assign_idx[None, :] < assign_idx[:, None])
    slot_rank = jnp.sum(matches.astype(jnp.int32), axis=1)
    place = jnp.where(flat_route >= 0, flat_route * capacity + slot_rank, -1)
    slots = jnp.arange(expert_count * capacity, dtype=jnp.int32)
    placed = place.reshape(tok_count, top_count, 1) == slots
    weighted = jnp.sum(jnp.where(placed, gate_weights[:, :, None], 0.0), axis=1)
    chosen = jnp.any(placed, axis=1)
    holder = jnp.sum(
        jnp.where(chosen, jnp.arange(1, tok_count + 1, dtype=jnp.int32)[:, None], 0), axis=0
    ) - 1
    holders = lax.all_gather(holder, "grp", axis=0, tiled=False)
    first = lax.axis_index("grp") * (local * capacity)
    mine = lax.dynamic_slice(holders, (0, first), (n_groups, local * capacity))
    wanted = mine.reshape(n_groups, local, capacity).transpose(1, 0, 2).reshape(-1)
    wanted = wanted.reshape(local, 1, per_source)
    source_row = jnp.arange(per_source, dtype=jnp.int32) // capacity * tok_count
    wanted = jnp.where(wanted >= 0, wanted + source_row, -1)
    wanted = jnp.broadcast_to(wanted, (local, pieces, per_source)).reshape(-1)
    select = (wanted[:, None] == jnp.arange(n_groups * tok_count, dtype=jnp.int32)[None, :]).astype(bf16)

    kv_block = lax.all_gather(caches.reshape(cache_rows, -1), "ep", axis=0, tiled=True)
    attended = attention(q_raw, k_raw, v_raw, q_gain, k_gain, kv_block, lengths, cont_owner, cache_rows)
    projected = jnp.dot(
        lax.all_gather(attended, "grp", axis=0, tiled=True), out_weight, preferred_element_type=f32
    ).astype(bf16)
    attn_proj = lax.all_to_all(projected, "grp", split_axis=0, concat_axis=1, tiled=True)
    hidden_state = (residual.astype(f32) + attn_proj.astype(f32)).astype(bf16)
    moe_in = normed(hidden_state.astype(f32), moe_gain).astype(bf16)

    tokens = lax.all_gather(moe_in, "grp", axis=0, tiled=True)
    outgoing = jnp.dot(select, tokens, preferred_element_type=f32).astype(bf16)
    received = lax.all_to_all(
        outgoing.reshape(n_columns, per_source, model_width), "ep", split_axis=0, concat_axis=0, tiled=True
    )
    rows_in = received.reshape(-1, model_width)
    gate_act = jnp.dot(rows_in, w_in[0], preferred_element_type=f32)
    up_act = jnp.dot(rows_in, w_in[1], preferred_element_type=f32)
    inner_act = (jax.nn.silu(gate_act) * up_act).astype(bf16)
    partial_out = jnp.dot(inner_act, w_down, preferred_element_type=f32).astype(bf16)
    returned = lax.all_to_all(
        partial_out.reshape(n_columns, per_source, model_width), "ep", split_axis=0, concat_axis=0, tiled=True
    ).reshape(-1, model_width)
    in_row = jnp.arange(n_columns * per_source, dtype=jnp.int32)
    in_slot = in_row % per_source
    target = (
        in_slot // capacity * (local * capacity)
        + in_row // (pieces * per_source) * capacity
        + in_slot % capacity
    )
    out_row = jnp.arange(n_groups * local * capacity, dtype=jnp.int32)
    gather_sum = (out_row[:, None] == target[None, :]).astype(bf16)
    summed = jnp.dot(gather_sum, returned, preferred_element_type=f32).astype(bf16)
    expert_out = lax.all_to_all(summed, "grp", split_axis=0, concat_axis=0, tiled=True)
    moe_out = jnp.dot(weighted, expert_out.astype(f32), precision=lax.Precision.HIGHEST)
    mixed = jnp.where(live_rows[:, None], hidden_state.astype(f32) + moe_out, 0.0)
    return mixed.astype(bf16)


def solution(mesh):
    in_specs = (
        P(("grp", "ep"), None),
        P(("grp", "ep"), None),
        P(("grp", "ep"), None),
        P(),
        P(),
        P("grp", "ep", None, None, None),
        P("grp", "ep"),
        P("grp", "ep"),
        P(None, "grp"),
        P(("grp", "ep"), None),
        P(),
        P(("grp", "ep"), None),
        P(("grp", "ep"), None),
        P(None, None, ("grp", "ep")),
        P(("grp", "ep"), None),
    )
    out_specs = P(("grp", "ep"), None)
    return jax.shard_map(
        per_device, mesh=mesh, in_specs=in_specs, out_specs=out_specs, check_vma=False
    )
```

time: 656 us -> 468 us (0.71)
  blocking collectives: 405 us -> 129 us
  waiting for transfers between devices: 138 us -> 276 us
  local copies, waits for them, and re-layouts: 62.1 us -> 4.4 us
  starting transfers between devices: 4.46 us -> 17.6 us
  other arithmetic: 11.5 us -> 2.45 us
    all_to_all x4 -> x2, blocking collectives: 405 us -> 114 us  [the longest x1 102 us: per_device(): lax.all_to_all(outgoing.reshape(n_columns, per_source, model_width), 'ep'...]
    all_to_all x1 -> x2, waiting for transfers between devices: 7.6 us -> 120 us  [the longest x1 92.7 us: per_device(): lax.all_to_all(partial_out.reshape(n_columns, per_source, model_width), '...]
    all_gather x1 -> x2, waiting for transfers between devices: 85.9 us -> 111 us  [the longest x1 89 us: per_device(): lax.all_gather(caches.reshape(cache_rows, -1), 'ep', axis=0, tiled=True)]
    all_to_all x4 -> x0, local copies, waits for them, and re-layouts: 24.9 us -> none  [the longest x1 6.47 us: per_device(): lax.all_to_all(outgoing, 'grp', split_axis=0, concat_axis=0, tiled=True)]
    all_gather x0 -> x1, blocking collectives: none -> 14.7 us  [per_device(): holders = lax.all_gather(holder, 'grp', axis=0, tiled=False)]
    reshape x4 -> x1, local copies, waits for them, and re-layouts: 16.3 us -> 1.71 us  [per_device(): caches.reshape(cache_rows, -1)]
    all_to_all x1 -> x2, starting transfers between devices: 4.42 us -> 17.5 us  [the longest x1 9.32 us: per_device(): lax.all_to_all(summed, 'grp', split_axis=0, concat_axis=0, tiled=True)]
    all_gather x1 -> x0, local copies, waits for them, and re-layouts: 11.2 us -> none  [per_device(): kv_block = lax.all_gather(caches[0], 'ep', axis=0, tiled=True)]
  transfers between devices with their start and end apart: 3 -> 5, of which waited for: 3 -> 5; matrix products, arithmetic and copies ran while one was open for 1% -> 0% of each run, Pallas kernels for 0% -> 0%
where the time goes in v1:
time: 468 us; the launch traced here: 467 us
  waiting for transfers between devices  276 us (59%)
  blocking collectives  129 us (28%)
  matrix products  19 us (4%)
  starting transfers between devices  17.6 us (4%)
  between operations  14.5 us (3%)
    all_to_all x1, blocking collectives, per_device(): lax.all_to_all(outgoing.reshape(n_columns, per_source, model_width), 'ep'...  102 us
    all_to_all x1, waiting for transfers between devices, per_device(): lax.all_to_all(partial_out.reshape(n_columns, per_source, model_width), '...  92.7 us
    all_gather x1, waiting for transfers between devices, per_device(): lax.all_gather(caches.reshape(cache_rows, -1), 'ep', axis=0, tiled=True)  89 us
    all_gather x1, waiting for transfers between devices, per_device(): lax.all_gather(attended, 'grp', axis=0, tiled=True)  44.1 us
    all_to_all x1, waiting for transfers between devices, per_device(): lax.all_to_all(summed, 'grp', split_axis=0, concat_axis=0, tiled=True)  27.8 us
    all_gather x1, waiting for transfers between devices, per_device(): tokens = lax.all_gather(moe_in, 'grp', axis=0, tiled=True)  22.2 us
    all_gather x1, blocking collectives, per_device(): holders = lax.all_gather(holder, 'grp', axis=0, tiled=False)  14.7 us
    all_to_all x1, blocking collectives, per_device(): lax.all_to_all(projected, 'grp', split_axis=0, concat_axis=1, tiled=True)  12 us
  transfers between devices with their start and end apart: 5, of which 5 were waited for; matrix products, arithmetic and copies ran while one was open for 0% of the time, Pallas kernels for 0%

profile of v1, /device:TPU:1, one launch (start us, length us, event | category | flops | bytes accessed | tf_op | source)
XLA Modules:
  0.0 467.0 jit_solution(9097992012947325543)
XLA Ops:
  6.5 1.7 reshape.169
  9.7 0.1 fusion.43
  9.8 0.7 pad_maximum_fusion
  10.5 89.0 %all-gather.6.cloned.1.call-done.kv_ref = bf16[1024,2048]{1,0:T(8,128)(2,1)} async-done(((bf16[32,2048]{1,0:T(8,128)(2,1)}), bf16[1024,2048]{1,0:T(8,128)(2,1)}) %all-gather.6.cloned.1.call-update) | async-done | bytes 4194320 | tf_op jit(solution)/shard_map/all_gather | solution.py:146
  99.5 4.6 shard_map.145
  104.1 44.1 %all-gather.8.cloned.1.call-done = bf16[256,4096]{1,0:T(8,128)(2,1)} async-done(((bf16[16,4096]{1,0:T(8,128)(2,1)}), bf16[256,4096]{1,0:T(8,128)(2,1)}) %all-gather.8.cloned.1.call-update) | async-done | bytes 2097168 | tf_op jit(solution)/shard_map/all_gather | solution.py:149
  148.3 2.3 convolution_convert_fusion.3
  150.6 12.0 %all_to_all.35 = bf16[16,16,128]{2,1,0:T(8,128)(2,1)S(1)} all-to-all(bf16[16,16,128]{2,1,0:T(8,128)(2,1)S(1)} %bitcast.46), channel_id=1, replica_groups=mesh['grp'=16,'ep'=32] {'grp'}, dimensions={0} | all-to-all | bytes 131072 | tf_op jit(solution)/shard_map/all_to_all | solution.py:151
  162.6 0.1 fusion.18
  162.7 0.7 fusion.20
  163.6 0.1 eq.59
  163.7 0.2 convert_reduce_fusion
  163.9 0.1 reduce_sum.39
  164.1 0.1 fusion.22
  164.2 0.1 select_reduce_fusion.1
  164.3 14.7 %all-gather.1 = s32[16,1,256]{2,1,0:T(1,128)S(1)} all-gather(s32[1,1,256]{2,1,0:T(1,128)S(1)} %bitcast.49), channel_id=2, replica_groups=mesh['grp'=16,'ep'=32] {'grp'}, dimensions={0}, use_global_device_ids=true | all-gather | bytes 17408 | tf_op jit(solution)/shard_map/all_gather | solution.py:136
  179.0 0.1 constant_dynamic-slice_fusion
  179.2 0.1 copy.40
  179.4 0.1 eq.69
  179.5 22.2 %all-gather.10.cloned.1.call-done = bf16[256,2048]{1,0:T(8,128)(2,1)} async-done(((bf16[16,2048]{1,0:T(8,128)(2,1)}), bf16[256,2048]{1,0:T(8,128)(2,1)}) %all-gather.10.cloned.1.call-update) | async-done | bytes 1048592 | tf_op jit(solution)/shard_map/all_gather | solution.py:155
  201.8 2.5 convolution_convert_fusion.1
  204.3 101.8 %all_to_all.36 = bf16[32,32,2048]{2,1,0:T(8,128)(2,1)S(1)} all-to-all(bf16[32,32,2048]{2,1,0:T(8,128)(2,1)S(1)} %bitcast.41), channel_id=1, replica_groups=mesh['grp'=16,'ep'=32] {'ep'}, dimensions={0} | all-to-all | bytes 8388608 | tf_op jit(solution)/shard_map/all_to_all | solution.py:157
  306.1 1.9 copy-done.1
  308.0 1.5 fusion.5
  309.6 7.1 %convolution_convert_fusion = bf16[1024,2048]{1,0:T(8,128)(2,1)} fusion(bf16[192,2048]{1,0:T(8,128)(2,1)S(1)} %copy-done.7, bf16[1024,2048]{1,0:T(8,128)(2,1)} %bitcast.44, bf16[2,2048,192]{1,2,0:T(8,128)(2,1)} %param.28, f32[1024,192]{0,1:T(8,128)S(1)} %fusion.5), kind=kOutput, calls=%fused_computation | convolution fusion | flops 1613889536 | bytes 10747904 | tf_op jit(solution)/shard_map/dot_general | solution.py:164
  316.7 8.2 %all-to-all-start.2 = ((bf16[32,32,2048]{2,1,0:T(8,128)(2,1)}), bf16[32,32,2048]{2,1,0:T(8,128)(2,1)}, u32[]{:S(2)}, u32[]{:S(2)}) async-start(bf16[32,32,2048]{2,1,0:T(8,128)(2,1)} %bitcast.42), calls=%async_computation.2 | async-start | bytes 8388608 | tf_op jit(solution)/shard_map/all_to_all | solution.py:165
  324.9 92.7 %all-to-all-done.2 = bf16[32,32,2048]{2,1,0:T(8,128)(2,1)} async-done(((bf16[32,32,2048]{2,1,0:T(8,128)(2,1)}), bf16[32,32,2048]{2,1,0:T(8,128)(2,1)}, u32[]{:S(2)}, u32[]{:S(2)}) %all-to-all-start.2) | async-done | bytes 4194336 | tf_op jit(solution)/shard_map/all_to_all | solution.py:165
  417.6 4.4 convolution_convert_fusion.2
  422.0 9.3 %all-to-all-start.3 = ((bf16[16,16,2048]{2,1,0:T(8,128)(2,1)}), bf16[16,16,2048]{2,1,0:T(8,128)(2,1)S(1)}, u32[]{:S(2)}, u32[]{:S(2)}) async-start(bf16[16,16,2048]{2,1,0:T(8,128)(2,1)} %bitcast.15), calls=%async_computation.3 | async-start | bytes 2097152 | tf_op jit(solution)/shard_map/all_to_all | solution.py:178
  431.4 0.1 select_reduce_fusion
  431.6 27.8 %all-to-all-done.3 = bf16[16,16,2048]{2,1,0:T(8,128)(2,1)S(1)} async-done(((bf16[16,16,2048]{2,1,0:T(8,128)(2,1)}), bf16[16,16,2048]{2,1,0:T(8,128)(2,1)S(1)}, u32[]{:S(2)}, u32[]{:S(2)}) %all-to-all-start.3) | async-done | bytes 1048608 | tf_op jit(solution)/shard_map/all_to_all | solution.py:178
  459.3 1.2 fusion.1
  (37 shorter events, 0.7 us)
Async XLA Ops:
  6.5 141.7 %copy-start = (bf16[4096,128]{1,0:T(8,128)(2,1)S(1)}, bf16[4096,128]{1,0:T(8,128)(2,1)}, u32[]{:S(2)}) copy-start(bf16[4096,128]{1,0:T(8,128)(2,1)} %param.23) | copy-start | bytes 3145732
  6.5 156.0 %copy-start.2 = (bf16[16,2048]{1,0:T(8,128)(2,1)S(1)}, bf16[16,2048]{1,0:T(8,128)(2,1)}, u32[]{:S(2)}) copy-start(bf16[16,2048]{1,0:T(8,128)(2,1)} %param.24) | copy-start | bytes 196612
  6.5 93.0 %all-gather.6.cloned.1.call-start = ((), (), s32[]{:S(2)}) async-start(), calls=%async_computation.4 | async-start | bytes 4325376 | tf_op jit(solution)/shard_map/all_gather | solution.py:146
  8.3 154.4 %copy-start.3 = (f32[2048]{0:T(1024)S(1)}, f32[2048]{0:T(1024)}, u32[]{:S(2)}) copy-start(f32[2048]{0:T(1024)} %param.25) | copy-start | bytes 24580
  8.3 140.0 %all-gather.8.cloned.1.call-start = ((), (), s32[]{:S(2)}) async-start(), calls=%async_computation.5 | async-start | bytes 2228224 | tf_op jit(solution)/shard_map/all_gather | solution.py:149
  99.5 64.0 %copy-start.4 = (s32[16,8]{0,1:T(8,128)S(1)}, s32[16,8]{0,1:T(8,128)}, u32[]{:S(2)}) copy-start(s32[16,8]{0,1:T(8,128)} %param.26) | copy-start | bytes 1540
  104.1 97.7 %all-gather.10.cloned.1.call-start = ((), (), s32[]{:S(2)}) async-start(), calls=%async_computation.6 | async-start | bytes 1114112 | tf_op jit(solution)/shard_map/all_gather | solution.py:155
  204.3 103.7 %copy-start.6 = (bf16[2,2048,192]{1,2,0:T(8,128)(2,1)S(1)}, bf16[2,2048,192]{1,2,0:T(8,128)(2,1)}, u32[]{:S(2)}) copy-start(bf16[2,2048,192]{1,2,0:T(8,128)(2,1)} %param.28) | copy-start | bytes 4718596
  306.1 1.9 copy-start.1
  306.1 3.5 copy-start.7
  316.7 100.9 %all-to-all-start.2 = ((bf16[32,32,2048]{2,1,0:T(8,128)(2,1)}), bf16[32,32,2048]{2,1,0:T(8,128)(2,1)}, u32[]{:S(2)}, u32[]{:S(2)}) async-start(bf16[32,32,2048]{2,1,0:T(8,128)(2,1)} %bitcast.42), calls=%async_computation.2 | async-start | bytes 8388608 | tf_op jit(solution)/shard_map/all_to_all | solution.py:165
  417.6 13.7 %copy-start.5 = (f32[16,8]{0,1:T(8,128)S(1)}, f32[16,8]{0,1:T(8,128)}, u32[]{:S(2)}) copy-start(f32[16,8]{0,1:T(8,128)} %param.27) | copy-start | bytes 1540
  422.0 37.3 %all-to-all-start.3 = ((bf16[16,16,2048]{2,1,0:T(8,128)(2,1)}), bf16[16,16,2048]{2,1,0:T(8,128)(2,1)S(1)}, u32[]{:S(2)}, u32[]{:S(2)}) async-start(bf16[16,16,2048]{2,1,0:T(8,128)(2,1)} %bitcast.15), calls=%async_computation.3 | async-start | bytes 2097152 | tf_op jit(solution)/shard_map/all_to_all | solution.py:178
Sparse Core Ops, SparseCore 0:
  10.5 88.9 all-gather.5
  104.2 44.0 all-gather.7
  163.6 38.1 all-gather.9

commit v2 on v1

--- a/solution.py
+++ b/solution.py
@@ -27,7 +27,7 @@
 
 
 def attention_body(
-    kv_heads, cache_rows, len_ref, own_ref, q_ref, k_ref, v_ref, qg_ref, kg_ref, cos_ref, sin_ref, kv_ref, out_ref
+    kv_heads, cache_rows, len_ref, own_ref, q_ref, k_ref, v_ref, qg_ref, kg_ref, cos_ref, sin_ref, kv_ref, tag_ref, out_ref
 ):
     tok_count = q_ref.shape[0]
     hd = qg_ref.shape[1]
@@ -52,6 +52,7 @@
     def weighed(queries, keys):
         return jnp.exp(lax.dot_general(queries, keys, contract, preferred_element_type=f32) * scaling)
 
+    out_ref[:, pl.ds(q_ref.shape[1], tag_ref.shape[1])] = tag_ref[...]
     for h in range(kv_heads):
         span = pl.ds(h * hd, hd)
         queries = jnp.concatenate(
@@ -77,7 +78,7 @@
             out_ref[:, pl.ds((h * group + j) * hd, hd)] = result[j * tok_count : (j + 1) * tok_count]
 
 
-def attention(q_raw, k_raw, v_raw, q_gain, k_gain, kv_block, lengths, cont_owner, cache_rows):
+def attention(q_raw, k_raw, v_raw, q_gain, k_gain, kv_block, tag, lengths, cont_owner, cache_rows):
     hd = q_gain.shape[0]
     tok_count = q_raw.shape[0]
     position = (kv_block.shape[0] + cache_rows + jnp.arange(tok_count, dtype=jnp.int32)).astype(f32)
@@ -86,10 +87,10 @@
     smem = pl.BlockSpec(memory_space=pltpu.SMEM)
     return pl.pallas_call(
         functools.partial(attention_body, k_raw.shape[1] // hd, cache_rows),
-        out_shape=jax.ShapeDtypeStruct(q_raw.shape, bf16),
-        in_specs=[smem, smem] + [vmem] * 8,
+        out_shape=jax.ShapeDtypeStruct((tok_count, q_raw.shape[1] + tag.shape[1]), bf16),
+        in_specs=[smem, smem] + [vmem] * 9,
         out_specs=vmem,
-    )(lengths, cont_owner, q_raw, k_raw, v_raw, q_gain[None], k_gain[None], cosine, sine, kv_block)
+    )(lengths, cont_owner, q_raw, k_raw, v_raw, q_gain[None], k_gain[None], cosine, sine, kv_block, tag)
 
 
 def per_device(
@@ -112,14 +113,28 @@
     n_groups = lax.axis_size("grp")
     n_columns = lax.axis_size("ep")
     tok_count, model_width = residual.shape
+    heads_width = q_raw.shape[1]
     cache_rows = caches.shape[1]
     top_count = routes.shape[1]
     pieces = 4
+    cores = 2
+    half = model_width // cores
     expert_count = n_groups * n_columns // pieces
     local = expert_count // n_groups
     capacity = 2
+    group_slots = local * capacity
     per_source = n_groups * capacity
+    core = lax.axis_index("grp") % cores
     live_rows = jnp.arange(tok_count, dtype=jnp.int32) < lengths[0, 0]
+
+    trades = []
+    for g in range(n_groups):
+        for p in range(n_columns):
+            to = (g - g % 2 + p % 2) * n_columns + p - p % 2 + g % 2
+            trades.append((g * n_columns + p, to))
+    w_in = lax.ppermute(w_in, ("grp", "ep"), trades)
+    w_down = lax.ppermute(w_down, ("grp", "ep"), trades)
+    swap = [(g, g ^ 1) for g in range(n_groups)]
 
     flat_route = jnp.where(live_rows[:, None], routes, -1).reshape(-1)
     assign_idx = jnp.arange(flat_route.shape[0], dtype=jnp.int32)
@@ -133,50 +148,75 @@
     holder = jnp.sum(
         jnp.where(chosen, jnp.arange(1, tok_count + 1, dtype=jnp.int32)[:, None], 0), axis=0
     ) - 1
-    holders = lax.all_gather(holder, "grp", axis=0, tiled=False)
-    first = lax.axis_index("grp") * (local * capacity)
-    mine = lax.dynamic_slice(holders, (0, first), (n_groups, local * capacity))
-    wanted = mine.reshape(n_groups, local, capacity).transpose(1, 0, 2).reshape(-1)
-    wanted = wanted.reshape(local, 1, per_source)
-    source_row = jnp.arange(per_source, dtype=jnp.int32) // capacity * tok_count
-    wanted = jnp.where(wanted >= 0, wanted + source_row, -1)
-    wanted = jnp.broadcast_to(wanted, (local, pieces, per_source)).reshape(-1)
-    select = (wanted[:, None] == jnp.arange(n_groups * tok_count, dtype=jnp.int32)[None, :]).astype(bf16)
+    tag = jnp.pad(holder.reshape(n_groups, group_slots).astype(bf16), ((0, 0), (0, 128 - group_slots)))
 
     kv_block = lax.all_gather(caches.reshape(cache_rows, -1), "ep", axis=0, tiled=True)
-    attended = attention(q_raw, k_raw, v_raw, q_gain, k_gain, kv_block, lengths, cont_owner, cache_rows)
-    projected = jnp.dot(
-        lax.all_gather(attended, "grp", axis=0, tiled=True), out_weight, preferred_element_type=f32
-    ).astype(bf16)
+    kv_block, w_in, w_down = lax.optimization_barrier((kv_block, w_in, w_down))
+    own_at, other_at = core * half, (1 - core) * half
+    w_in_own = lax.dynamic_slice_in_dim(w_in, own_at, half, 1)
+    w_in_other = lax.dynamic_slice_in_dim(w_in, other_at, half, 1)
+    w_down_own = lax.dynamic_slice_in_dim(w_down, own_at, half, 1)
+    w_down_other = lax.dynamic_slice_in_dim(w_down, other_at, half, 1)
+    attended = attention(q_raw, k_raw, v_raw, q_gain, k_gain, kv_block, tag, lengths, cont_owner, cache_rows)
+    gathered = lax.all_gather(attended, "grp", axis=0, tiled=True)
+    projected = jnp.dot(gathered[:, :heads_width], out_weight, preferred_element_type=f32).astype(bf16)
     attn_proj = lax.all_to_all(projected, "grp", split_axis=0, concat_axis=1, tiled=True)
     hidden_state = (residual.astype(f32) + attn_proj.astype(f32)).astype(bf16)
     moe_in = normed(hidden_state.astype(f32), moe_gain).astype(bf16)
 
+    holders = gathered[:, heads_width : heads_width + group_slots].astype(jnp.int32)
+    holders = holders.reshape(n_groups, n_groups, group_slots)
+    mine = lax.dynamic_slice_in_dim(holders, lax.axis_index("grp") - core, cores, 1)
+    mine = mine.reshape(n_groups, cores, local, capacity).transpose(2, 1, 0, 3)
+    source_row = (jnp.arange(n_groups, dtype=jnp.int32) * tok_count)[:, None]
+    wanted = jnp.where(mine >= 0, mine + source_row, -1)
+    wanted = jnp.broadcast_to(wanted[:, None], (local, pieces // cores) + wanted.shape[1:]).reshape(-1)
+    select = (wanted[:, None] == jnp.arange(n_groups * tok_count, dtype=jnp.int32)[None, :]).astype(bf16)
+
     tokens = lax.all_gather(moe_in, "grp", axis=0, tiled=True)
-    outgoing = jnp.dot(select, tokens, preferred_element_type=f32).astype(bf16)
+    outgoing = jnp.dot(
+        select, lax.dynamic_slice_in_dim(tokens, own_at, half, 1), preferred_element_type=f32
+    ).astype(bf16)
     received = lax.all_to_all(
-        outgoing.reshape(n_columns, per_source, model_width), "ep", split_axis=0, concat_axis=0, tiled=True
-    )
-    rows_in = received.reshape(-1, model_width)
-    gate_act = jnp.dot(rows_in, w_in[0], preferred_element_type=f32)
-    up_act = jnp.dot(rows_in, w_in[1], preferred_element_type=f32)
-    inner_act = (jax.nn.silu(gate_act) * up_act).astype(bf16)
-    partial_out = jnp.dot(inner_act, w_down, preferred_element_type=f32).astype(bf16)
+        outgoing.reshape(n_columns, per_source, half), "ep", split_axis=0, concat_axis=0, tiled=True
+    ).reshape(-1, half)
+    partner = lax.ppermute(received, "grp", swap)
+
+    def project(which):
+        return jnp.dot(received, w_in_own[which], preferred_element_type=f32) + jnp.dot(
+            partner, w_in_other[which], preferred_element_type=f32
+        )
+
+    inner_act = (jax.nn.silu(project(0)) * project(1)).astype(bf16)
+    for_partner = jnp.dot(inner_act, w_down_other, preferred_element_type=f32).astype(bf16)
+    from_partner = lax.ppermute(for_partner, "grp", swap)
+    partial_out = jnp.dot(inner_act, w_down_own, preferred_element_type=f32)
+    partial_out = (partial_out + from_partner.astype(f32)).astype(bf16)
     returned = lax.all_to_all(
-        partial_out.reshape(n_columns, per_source, model_width), "ep", split_axis=0, concat_axis=0, tiled=True
-    ).reshape(-1, model_width)
+        partial_out.reshape(n_columns, per_source, half), "ep", split_axis=0, concat_axis=0, tiled=True
+    ).reshape(-1, half)
     in_row = jnp.arange(n_columns * per_source, dtype=jnp.int32)
-    in_slot = in_row % per_source
+    in_slot, in_column = in_row % per_source, in_row // per_source
     target = (
-        in_slot // capacity * (local * capacity)
-        + in_row // (pieces * per_source) * capacity
+        in_slot // capacity * (cores * group_slots)
+        + in_column % cores * group_slots
+        + in_column // pieces * capacity
         + in_slot % capacity
     )
-    out_row = jnp.arange(n_groups * local * capacity, dtype=jnp.int32)
+    out_row = jnp.arange(n_groups * cores * group_slots, dtype=jnp.int32)
     gather_sum = (out_row[:, None] == target[None, :]).astype(bf16)
     summed = jnp.dot(gather_sum, returned, preferred_element_type=f32).astype(bf16)
-    expert_out = lax.all_to_all(summed, "grp", split_axis=0, concat_axis=0, tiled=True)
-    moe_out = jnp.dot(weighted, expert_out.astype(f32), precision=lax.Precision.HIGHEST)
+    expert_out = lax.all_to_all(
+        summed.reshape(n_groups, cores * group_slots, half), "grp", split_axis=0, concat_axis=0, tiled=True
+    )
+    expert_out = expert_out.reshape(n_groups // cores, cores, cores * group_slots, half).astype(f32)
+    moe_out = jnp.concatenate(
+        [
+            jnp.dot(weighted, expert_out[:, c].reshape(-1, half), precision=lax.Precision.HIGHEST)
+            for c in range(cores)
+        ],
+        axis=1,
+    )
     mixed = jnp.where(live_rows[:, None], hidden_state.astype(f32) + moe_out, 0.0)
     return mixed.astype(bf16)
 

time: 468 us -> 383 us (0.82)
  blocking collectives: 129 us -> 68.7 us
  waiting for transfers between devices: 276 us -> 244 us
  starting transfers between devices: 17.6 us -> 26.5 us
    all_to_all x1, blocking collectives: 102 us -> 56.7 us  [per_device(): lax.all_to_all(outgoing.reshape(n_columns, per_source, half), 'ep', split...]
    all_to_all x2, waiting for transfers between devices: 120 us -> 76.6 us  [the longest x1 48.8 us: per_device(): lax.all_to_all(partial_out.reshape(n_columns, per_source, half), 'ep', sp...]
    all_gather x1, waiting for transfers between devices: 89 us -> 58 us  [per_device(): lax.all_gather(caches.reshape(cache_rows, -1), 'ep', axis=0, tiled=True)]
    ppermute x0 -> x4, waiting for transfers between devices: none -> 27 us  [the longest x1 22.2 us: per_device(): w_down = lax.ppermute(w_down, ('grp', 'ep'), trades)]
    all_gather x1, waiting for transfers between devices: 22.2 us -> 37.7 us  [per_device(): tokens = lax.all_gather(moe_in, 'grp', axis=0, tiled=True)]
    ppermute x0 -> x4, starting transfers between devices: none -> 15.1 us  [the longest x1 6.28 us: per_device(): partner = lax.ppermute(received, 'grp', swap)]
    all_gather x1 -> x0, blocking collectives: 14.7 us -> none  [per_device(): holders = lax.all_gather(holder, 'grp', axis=0, tiled=False)]
    all_to_all x2, starting transfers between devices: 17.5 us -> 11.3 us  [the longest x1 6.49 us: per_device(): lax.all_to_all(summed.reshape(n_groups, cores * group_slots, half), 'grp'...]
  transfers between devices with their start and end apart: 5 -> 9, of which waited for: 5 -> 8; matrix products, arithmetic and copies ran while one was open for 0% -> 2% of each run, Pallas kernels for 0% -> 0%
where the time goes in v2:
time: 383 us
  waiting for transfers between devices  244 us (64%)
  blocking collectives  68.7 us (18%)
  starting transfers between devices  26.5 us (7%)
  matrix products  17.7 us (5%)
  between operations  14.7 us (4%)
  Pallas kernels  4.42 us (1%)
  local copies, waits for them, and re-layouts  3.97 us (1%)
    all_gather x1, waiting for transfers between devices, per_device(): lax.all_gather(caches.reshape(cache_rows, -1), 'ep', axis=0, tiled=True)  58 us
    all_to_all x1, blocking collectives, per_device(): lax.all_to_all(outgoing.reshape(n_columns, per_source, half), 'ep', split...  56.7 us
    all_to_all x1, waiting for transfers between devices, per_device(): lax.all_to_all(partial_out.reshape(n_columns, per_source, half), 'ep', sp...  48.8 us
    all_gather x1, waiting for transfers between devices, per_device(): gathered = lax.all_gather(attended, 'grp', axis=0, tiled=True)  44.2 us
    all_gather x1, waiting for transfers between devices, per_device(): tokens = lax.all_gather(moe_in, 'grp', axis=0, tiled=True)  37.7 us
    all_to_all x1, waiting for transfers between devices, per_device(): lax.all_to_all(summed.reshape(n_groups, cores * group_slots, half), 'grp'...  27.8 us
    ppermute x1, waiting for transfers between devices, per_device(): w_down = lax.ppermute(w_down, ('grp', 'ep'), trades)  22.2 us
    all_to_all x1, blocking collectives, per_device(): lax.all_to_all(projected, 'grp', split_axis=0, concat_axis=1, tiled=True)  12 us
  transfers between devices with their start and end apart: 9, of which 8 were waited for; matrix products, arithmetic and copies ran while one was open for 2% of the time, Pallas kernels for 0%

profile of v2, /device:TPU:1, one launch (start us, length us, event | category | flops | bytes accessed | tf_op | source)
XLA Modules:
  0.0 382.6 jit_solution(4153638476917122824)
XLA Ops:
  6.5 1.7 reshape.164
  8.3 4.6 %collective-permute-start = (bf16[2,2048,192]{1,2,0:T(8,128)(2,1)}, bf16[2,2048,192]{1,2,0:T(8,128)(2,1)S(1)}, u32[]{:S(2)}, u32[]{:S(2)}) collective-permute-start(bf16[2,2048,192]{1,2,0:T(8,128)(2,1)} %param.28), channel_id=1, source_target_pairs={{0,0},{1,32},{2,2},{3,34},{4,4},{5,36},{6,6},{7,38},{8,8},{9,40},{... | collective-permute-start | bytes 4718600 | tf_op jit(solution)/shard_map/ppermute | solution.py:135
  12.9 1.9 collective-permute-start.1
  15.5 0.8 copy.26
  17.8 0.6 pad.4.tag_ref
  18.5 0.7 pad_maximum_fusion
  19.2 22.2 %collective-permute-done.1 = bf16[192,2048]{1,0:T(8,128)(2,1)S(1)} collective-permute-done((bf16[192,2048]{1,0:T(8,128)(2,1)}, bf16[192,2048]{1,0:T(8,128)(2,1)S(1)}, u32[]{:S(2)}, u32[]{:S(2)}) %collective-permute-start.1) | collective-permute-done | bytes 786464 | tf_op jit(solution)/shard_map/ppermute | solution.py:136
  41.4 58.0 %all-gather.4.cloned.1.call-done.kv_ref = bf16[1024,2048]{1,0:T(8,128)(2,1)} async-done(((bf16[32,2048]{1,0:T(8,128)(2,1)}), bf16[1024,2048]{1,0:T(8,128)(2,1)}) %all-gather.4.cloned.1.call-update) | async-done | bytes 4194320 | tf_op jit(solution)/shard_map/all_gather | solution.py:153
  99.4 4.4 %shard_map.145 = bf16[16,4224]{1,0:T(8,128)(2,1)} custom-call(s32[1,1]{1,0:T(1,128)} %copy.35.len_ref, s32[1,1]{1,0:T(1,128)S(6)} %copy.36.own_ref, bf16[16,4096]{1,0:T(8,128)(2,1)} %q_ref.1, bf16[16,512]{1,0:T(8,128)(2,1)} %k_ref.1, bf16[16,512]{1,0:T(8,128)(2,1)} %v_ref.1, f32[1,128]{1,0:T(1,128)} %bitcast.65, f32[1,128]{1,0:T(1,128)} %bitcast.66, ...), custom_call_target="tpu_custom_call" | custom-call | tf_op jit(solution)/shard_map/pallas_call | solution.py:88
  103.9 44.2 %all-gather.6.cloned.1.call-done = bf16[256,4224]{1,0:T(8,128)(2,1)} async-done(((bf16[16,4224]{1,0:T(8,128)(2,1)}), bf16[256,4224]{1,0:T(8,128)(2,1)}) %all-gather.6.cloned.1.call-update) | async-done | bytes 2162704 | tf_op jit(solution)/shard_map/all_gather | solution.py:161
  148.1 2.3 fusion.6
  150.4 12.0 %all_to_all.28 = bf16[16,16,128]{2,1,0:T(8,128)(2,1)S(1)} all-to-all(bf16[16,16,128]{2,1,0:T(8,128)(2,1)S(1)} %bitcast.63), channel_id=1, replica_groups=mesh['grp'=16,'ep'=32] {'grp'}, dimensions={0} | all-to-all | bytes 131072 | tf_op jit(solution)/shard_map/all_to_all | solution.py:163
  162.6 0.7 fusion.18
  163.9 37.7 %all-gather.8.cloned.1.call-done = bf16[256,2048]{1,0:T(8,128)(2,1)} async-done(((bf16[16,2048]{1,0:T(8,128)(2,1)}), bf16[256,2048]{1,0:T(8,128)(2,1)}) %all-gather.8.cloned.1.call-update) | async-done | bytes 1048592 | tf_op jit(solution)/shard_map/all_gather | solution.py:176
  201.6 1.8 convolution_convert_fusion.1
  203.4 56.7 %all_to_all.29 = bf16[32,32,1024]{2,1,0:T(8,128)(2,1)S(1)} all-to-all(bf16[32,32,1024]{2,1,0:T(8,128)(2,1)S(1)} %bitcast.56), channel_id=1, replica_groups=mesh['grp'=16,'ep'=32] {'ep'}, dimensions={0} | all-to-all | bytes 4194304 | tf_op jit(solution)/shard_map/all_to_all | solution.py:180
  260.1 6.3 %collective-permute-start.2 = (bf16[1024,1024]{1,0:T(8,128)(2,1)S(1)}, bf16[1024,1024]{1,0:T(8,128)(2,1)}, u32[]{:S(2)}, u32[]{:S(2)}) collective-permute-start(bf16[1024,1024]{1,0:T(8,128)(2,1)S(1)} %bitcast.53), channel_id=1, source_target_pairs={{0,32},{32,0},{64,96},{96,64},{128,160},{160,128},{192,224},{224,1... | collective-permute-start | bytes 6291464 | tf_op jit(solution)/shard_map/ppermute | solution.py:183
  266.4 2.0 fusion.13
  268.4 0.8 fusion.12
  269.2 1.1 collective-permute-done.2
  270.3 2.4 convolution_add_fusion.1
  272.7 2.6 fusion.5
  275.4 0.7 convolution_convert_fusion
  276.1 2.3 collective-permute-start.3
  278.4 3.8 collective-permute-done.3
  282.2 2.1 add_convert_fusion
  284.3 4.8 %all-to-all-start.2 = ((bf16[32,32,1024]{2,1,0:T(8,128)(2,1)}), bf16[32,32,1024]{2,1,0:T(8,128)(2,1)S(1)}, u32[]{:S(2)}, u32[]{:S(2)}) async-start(bf16[32,32,1024]{2,1,0:T(8,128)(2,1)} %bitcast.14), calls=%async_computation.2 | async-start | bytes 4194304 | tf_op jit(solution)/shard_map/all_to_all | solution.py:195
  289.1 48.8 %all-to-all-done.2 = bf16[32,32,1024]{2,1,0:T(8,128)(2,1)S(1)} async-done(((bf16[32,32,1024]{2,1,0:T(8,128)(2,1)}), bf16[32,32,1024]{2,1,0:T(8,128)(2,1)S(1)}, u32[]{:S(2)}, u32[]{:S(2)}) %all-to-all-start.2) | async-done | bytes 2097184 | tf_op jit(solution)/shard_map/all_to_all | solution.py:195
  337.9 2.2 fusion.3
  340.2 6.5 %all-to-all-start.3 = ((bf16[16,32,1024]{2,1,0:T(8,128)(2,1)}), bf16[16,32,1024]{2,1,0:T(8,128)(2,1)S(1)}, u32[]{:S(2)}, u32[]{:S(2)}) async-start(bf16[16,32,1024]{2,1,0:T(8,128)(2,1)} %bitcast.61), calls=%async_computation.3 | async-start | bytes 2097152 | tf_op jit(solution)/shard_map/all_to_all | solution.py:209
  346.9 27.8 %all-to-all-done.3 = bf16[16,32,1024]{2,1,0:T(8,128)(2,1)S(1)} async-done(((bf16[16,32,1024]{2,1,0:T(8,128)(2,1)}), bf16[16,32,1024]{2,1,0:T(8,128)(2,1)S(1)}, u32[]{:S(2)}, u32[]{:S(2)}) %all-to-all-start.3) | async-done | bytes 1048608 | tf_op jit(solution)/shard_map/all_to_all | solution.py:209
  375.4 0.7 fusion.20
  (54 shorter events, 2.7 us)
Async XLA Ops:
  6.5 141.6 %copy-start = (bf16[4096,128]{1,0:T(8,128)(2,1)S(1)}, bf16[4096,128]{1,0:T(8,128)(2,1)}, u32[]{:S(2)}) copy-start(bf16[4096,128]{1,0:T(8,128)(2,1)} %param.23) | copy-start | bytes 3145732
  6.5 92.9 %all-gather.4.cloned.1.call-start = ((), (), s32[]{:S(2)}) async-start(), calls=%async_computation.4 | async-start | bytes 4325376 | tf_op jit(solution)/shard_map/all_gather | solution.py:153
  8.3 139.8 %all-gather.6.cloned.1.call-start = ((), (), s32[]{:S(2)}) async-start(), calls=%async_computation.5 | async-start | bytes 2297856 | tf_op jit(solution)/shard_map/all_gather | solution.py:161
  8.3 33.1 %collective-permute-start = (bf16[2,2048,192]{1,2,0:T(8,128)(2,1)}, bf16[2,2048,192]{1,2,0:T(8,128)(2,1)S(1)}, u32[]{:S(2)}, u32[]{:S(2)}) collective-permute-start(bf16[2,2048,192]{1,2,0:T(8,128)(2,1)} %param.28), channel_id=1, source_target_pairs={{0,0},{1,32},{2,2},{3,34},{4,4},{5,36},{6,6},{7,38},{8,8},{9,40},{... | collective-permute-start | bytes 4718600 | tf_op jit(solution)/shard_map/ppermute | solution.py:135
  12.9 28.5 %collective-permute-start.1 = (bf16[192,2048]{1,0:T(8,128)(2,1)}, bf16[192,2048]{1,0:T(8,128)(2,1)S(1)}, u32[]{:S(2)}, u32[]{:S(2)}) collective-permute-start(bf16[192,2048]{1,0:T(8,128)(2,1)} %param.29), channel_id=1, source_target_pairs={{0,0},{1,32},{2,2},{3,34},{4,4},{5,36},{6,6},{7,38},{8,8},{9,40},{... | collective-permute-start | bytes 2359304 | tf_op jit(solution)/shard_map/ppermute | solution.py:136
  41.4 62.4 %copy-start.3 = (bf16[192,2048]{1,0:T(8,128)(2,1)}, bf16[192,2048]{1,0:T(8,128)(2,1)S(1)}, u32[]{:S(2)}) copy-start(bf16[192,2048]{1,0:T(8,128)(2,1)S(1)} %collective-permute-done.1) | copy-start | bytes 2359300
  41.4 62.4 %copy-start.1 = (bf16[2,2048,192]{1,2,0:T(8,128)(2,1)}, bf16[2,2048,192]{1,2,0:T(8,128)(2,1)S(1)}, u32[]{:S(2)}) copy-start(bf16[2,2048,192]{1,2,0:T(8,128)(2,1)S(1)} %collective-permute-done) | copy-start | bytes 4718596
  103.8 58.6 %copy-start.5 = (bf16[16,2048]{1,0:T(8,128)(2,1)S(1)}, bf16[16,2048]{1,0:T(8,128)(2,1)}, u32[]{:S(2)}) copy-start(bf16[16,2048]{1,0:T(8,128)(2,1)} %param.24) | copy-start | bytes 196612
  103.9 58.7 %copy-start.6 = (f32[2048]{0:T(1024)S(1)}, f32[2048]{0:T(1024)}, u32[]{:S(2)}) copy-start(f32[2048]{0:T(1024)} %param.25) | copy-start | bytes 24580
  103.9 97.7 %all-gather.8.cloned.1.call-start = ((), (), s32[]{:S(2)}) async-start(), calls=%async_computation.6 | async-start | bytes 1114112 | tf_op jit(solution)/shard_map/all_gather | solution.py:176
  148.1 15.3 %slice-start = ((bf16[256,4224]{1,0:T(8,128)(2,1)}), bf16[256,16]{1,0:T(8,128)(2,1)S(1)}, s32[]{:S(2)}) async-start(bf16[256,4224]{1,0:T(8,128)(2,1)} %all-gather.6.cloned.1.call-done), calls=%async_computation.7 | async-start | bytes 131072 | tf_op jit(solution)/shard_map/slice | solution.py:167
  260.1 10.2 %collective-permute-start.2 = (bf16[1024,1024]{1,0:T(8,128)(2,1)S(1)}, bf16[1024,1024]{1,0:T(8,128)(2,1)}, u32[]{:S(2)}, u32[]{:S(2)}) collective-permute-start(bf16[1024,1024]{1,0:T(8,128)(2,1)S(1)} %bitcast.53), channel_id=1, source_target_pairs={{0,32},{32,0},{64,96},{96,64},{128,160},{160,128},{192,224},{224,1... | collective-permute-start | bytes 6291464 | tf_op jit(solution)/shard_map/ppermute | solution.py:183
  266.4 2.0 copy-start.2
  272.7 2.6 copy-start.4
  276.1 6.1 %collective-permute-start.3 = (bf16[1024,1024]{1,0:T(8,128)(2,1)S(1)}, bf16[1024,1024]{1,0:T(8,128)(2,1)S(1)}, u32[]{:S(2)}, u32[]{:S(2)}) collective-permute-start(bf16[1024,1024]{1,0:T(8,128)(2,1)S(1)} %convolution_convert_fusion), channel_id=1, source_target_pairs={{0,32},{32,0},{64,96},{96,64},{128,160},{160,128},{192,224},{224,1... | collective-permute-start | bytes 6291464 | tf_op jit(solution)/shard_map/ppermute | solution.py:192
  284.3 53.7 %all-to-all-start.2 = ((bf16[32,32,1024]{2,1,0:T(8,128)(2,1)}), bf16[32,32,1024]{2,1,0:T(8,128)(2,1)S(1)}, u32[]{:S(2)}, u32[]{:S(2)}) async-start(bf16[32,32,1024]{2,1,0:T(8,128)(2,1)} %bitcast.14), calls=%async_computation.2 | async-start | bytes 4194304 | tf_op jit(solution)/shard_map/all_to_all | solution.py:195
  340.2 6.5 %copy-start.7 = (f32[16,8]{0,1:T(8,128)S(1)}, f32[16,8]{0,1:T(8,128)}, u32[]{:S(2)}) copy-start(f32[16,8]{0,1:T(8,128)} %param.27) | copy-start | bytes 1540
  340.2 34.5 %all-to-all-start.3 = ((bf16[16,32,1024]{2,1,0:T(8,128)(2,1)}), bf16[16,32,1024]{2,1,0:T(8,128)(2,1)S(1)}, u32[]{:S(2)}, u32[]{:S(2)}) async-start(bf16[16,32,1024]{2,1,0:T(8,128)(2,1)} %bitcast.61), calls=%async_computation.3 | async-start | bytes 2097152 | tf_op jit(solution)/shard_map/all_to_all | solution.py:209
Sparse Core Ops, SparseCore 0:
  10.5 88.8 all-gather.3
  104.0 44.0 all-gather.5
  163.5 38.1 all-gather.7

commit v3 on v2

--- a/solution.py
+++ b/solution.py
@@ -24,6 +24,195 @@
     angles = position[:, None] * inv_freq[None, :]
     cosine, sine = jnp.cos(angles), jnp.sin(angles)
     return jnp.concatenate([cosine, cosine], -1), jnp.concatenate([-sine, sine], -1)
+
+
+MESH = pl.DeviceIdType.MESH
+
+
+class Flights:
+    def __init__(self, send_sems, recv_sems):
+        self.sems = send_sems, recv_sems
+        self.copies = []
+
+    def send(self, src, dst, device):
+        at = len(self.copies)
+        copy = pltpu.make_async_remote_copy(
+            src, dst, self.sems[0].at[at], self.sems[1].at[at], device_id=device, device_id_type=MESH
+        )
+        copy.start()
+        self.copies.append(copy)
+        return copy
+
+    def finish(self):
+        for copy in self.copies:
+            copy.wait_send()
+
+
+def greet(devices):
+    barrier = pltpu.get_barrier_semaphore()
+    for device in devices:
+        pl.semaphore_signal(barrier, inc=1, device_id=device, device_id_type=MESH)
+    pl.semaphore_wait(barrier, len(devices))
+
+
+def ring_order(n):
+    order = [0]
+    for step in range(1, n // 2 + 1):
+        order.append(-step)
+        if step < n - n // 2:
+            order.append(step)
+    return order
+
+
+def column_gather_body(columns, in_ref, out_ref, local_sem, send_sems, recv_sems):
+    g, p = lax.axis_index("grp"), lax.axis_index("ep")
+    n_x = lax.axis_size("ep") // columns
+    x, y = p // columns, p % columns
+    half = in_ref.shape[0] // 2
+    up = (g, x * columns + (y + 1) % columns)
+    down = (g, x * columns + (y + columns - 1) % columns)
+    right = (g, (x + 1) % n_x * columns + y)
+    left = (g, (x + n_x - 1) % n_x * columns + y)
+    greet([up, down, right, left])
+    flights = Flights(send_sems, recv_sems)
+    local = pltpu.make_async_copy(in_ref, out_ref.at[p], local_sem)
+    local.start()
+
+    def block(across, along):
+        return (x + across + n_x) % n_x * columns + (y + along + columns) % columns
+
+    coming, sideways = {}, []
+    order = ring_order(columns)
+    for along in order:
+        here = out_ref.at[block(0, along)]
+        if along == 0:
+            source = in_ref
+        else:
+            coming[along].wait_recv()
+            source = here
+        if along <= 0 and along - 1 in order:
+            coming[along - 1] = flights.send(source, here, up)
+        if along >= 0 and along + 1 in order:
+            coming[along + 1] = flights.send(source, here, down)
+        sideways.append((flights.send(source, here, right), flights.send(source, here, left)))
+    last = []
+    for along, (from_left, from_right) in zip(order, sideways):
+        from_left.wait_recv()
+        part = out_ref.at[block(-1, along), pl.ds(0, half)]
+        last.append(flights.send(part, part, right))
+        from_right.wait_recv()
+        part = out_ref.at[block(1, along), pl.ds(half, half)]
+        last.append(flights.send(part, part, left))
+    for copy in last:
+        copy.wait_recv()
+    local.wait()
+    flights.finish()
+
+
+def column_gather(rows, columns, n_columns):
+    count = columns - 1 + 4 * columns
+    vmem = pl.BlockSpec(memory_space=pltpu.VMEM)
+    gathered = pl.pallas_call(
+        functools.partial(column_gather_body, columns),
+        out_shape=jax.ShapeDtypeStruct((n_columns,) + rows.shape, rows.dtype),
+        in_specs=[vmem],
+        out_specs=vmem,
+        scratch_shapes=[
+            pltpu.SemaphoreType.DMA,
+            pltpu.SemaphoreType.DMA((count,)),
+            pltpu.SemaphoreType.DMA((count,)),
+        ],
+        compiler_params=pltpu.CompilerParams(collective_id=0, has_side_effects=True),
+        cost_estimate=pl.CostEstimate(flops=10**9, bytes_accessed=1 << 27, transcendentals=0),
+    )(rows)
+    return gathered.reshape(-1, rows.shape[1])
+
+
+def group_places():
+    g, p = lax.axis_index("grp"), lax.axis_index("ep")
+    depth = lax.axis_size("grp") // 2
+    z, core = g // 2, g % 2
+    up = ((z + 1) % depth * 2 + core, p)
+    down = ((z + depth - 1) % depth * 2 + core, p)
+    partner = (z * 2 + 1 - core, p)
+    return g, depth, z, core, up, down, partner
+
+
+def group_gather_body(in_ref, out_ref, local_sem, send_sems, recv_sems):
+    g, depth, z, core, up, down, partner = group_places()
+    greet([up, down, partner])
+    flights = Flights(send_sems, recv_sems)
+    local = pltpu.make_async_copy(in_ref, out_ref.at[g], local_sem)
+    local.start()
+    coming, handed = {}, []
+    order = ring_order(depth)
+    for along in order:
+        here = out_ref.at[(z + along + depth) % depth * 2 + core]
+        if along == 0:
+            source = in_ref
+        else:
+            coming[along].wait_recv()
+            source = here
+        if along <= 0 and along - 1 in order:
+            coming[along - 1] = flights.send(source, here, up)
+        if along >= 0 and along + 1 in order:
+            coming[along + 1] = flights.send(source, here, down)
+        handed.append(flights.send(source, here, partner))
+    for copy in handed:
+        copy.wait_recv()
+    local.wait()
+    flights.finish()
+
+
+def half_gather_body(in_ref, out_ref, local_sem, send_sems, recv_sems):
+    g, depth, z, core, up, down, partner = group_places()
+    half = out_ref.shape[2]
+    greet([up, down, partner])
+    flights = Flights(send_sems, recv_sems)
+    own = in_ref.at[:, pl.ds(pl.multiple_of(core * half, half), half)]
+    other = in_ref.at[:, pl.ds(pl.multiple_of((1 - core) * half, half), half)]
+    swapped = flights.send(other, out_ref.at[g], partner)
+    local = pltpu.make_async_copy(own, out_ref.at[g], local_sem)
+    local.start()
+    swapped.wait_recv()
+    local.wait()
+    coming = {}
+    order = ring_order(depth)
+    for along in order:
+        here = out_ref.at[pl.ds((z + along + depth) % depth * 2, 2)]
+        if along != 0:
+            coming[along].wait_recv()
+        if along <= 0 and along - 1 in order:
+            coming[along - 1] = flights.send(here, here, up)
+        if along >= 0 and along + 1 in order:
+            coming[along + 1] = flights.send(here, here, down)
+    flights.finish()
+
+
+def over_groups(body, count, width, collective_id, rows):
+    n_groups = lax.axis_size("grp")
+    vmem = pl.BlockSpec(memory_space=pltpu.VMEM)
+    gathered = pl.pallas_call(
+        body,
+        out_shape=jax.ShapeDtypeStruct((n_groups, rows.shape[0], width), rows.dtype),
+        in_specs=[vmem],
+        out_specs=vmem,
+        scratch_shapes=[
+            pltpu.SemaphoreType.DMA,
+            pltpu.SemaphoreType.DMA((count,)),
+            pltpu.SemaphoreType.DMA((count,)),
+        ],
+        compiler_params=pltpu.CompilerParams(collective_id=collective_id, has_side_effects=True),
+    )(rows)
+    return gathered.reshape(-1, width)
+
+
+def group_gather(rows):
+    return over_groups(group_gather_body, lax.axis_size("grp") - 1, rows.shape[1], 1, rows)
+
+
+def half_gather(rows):
+    return over_groups(half_gather_body, lax.axis_size("grp") // 2, rows.shape[1] // 2, 2, rows)
 
 
 def attention_body(
@@ -118,6 +307,7 @@
     top_count = routes.shape[1]
     pieces = 4
     cores = 2
+    ring_columns = 8
     half = model_width // cores
     expert_count = n_groups * n_columns // pieces
     local = expert_count // n_groups
@@ -150,7 +340,7 @@
     ) - 1
     tag = jnp.pad(holder.reshape(n_groups, group_slots).astype(bf16), ((0, 0), (0, 128 - group_slots)))
 
-    kv_block = lax.all_gather(caches.reshape(cache_rows, -1), "ep", axis=0, tiled=True)
+    kv_block = column_gather(caches.reshape(cache_rows, -1), ring_columns, n_columns)
     kv_block, w_in, w_down = lax.optimization_barrier((kv_block, w_in, w_down))
     own_at, other_at = core * half, (1 - core) * half
     w_in_own = lax.dynamic_slice_in_dim(w_in, own_at, half, 1)
@@ -158,7 +348,7 @@
     w_down_own = lax.dynamic_slice_in_dim(w_down, own_at, half, 1)
     w_down_other = lax.dynamic_slice_in_dim(w_down, other_at, half, 1)
     attended = attention(q_raw, k_raw, v_raw, q_gain, k_gain, kv_block, tag, lengths, cont_owner, cache_rows)
-    gathered = lax.all_gather(attended, "grp", axis=0, tiled=True)
+    gathered = group_gather(attended)
     projected = jnp.dot(gathered[:, :heads_width], out_weight, preferred_element_type=f32).astype(bf16)
     attn_proj = lax.all_to_all(projected, "grp", split_axis=0, concat_axis=1, tiled=True)
     hidden_state = (residual.astype(f32) + attn_proj.astype(f32)).astype(bf16)
@@ -173,10 +363,7 @@
     wanted = jnp.broadcast_to(wanted[:, None], (local, pieces // cores) + wanted.shape[1:]).reshape(-1)
     select = (wanted[:, None] == jnp.arange(n_groups * tok_count, dtype=jnp.int32)[None, :]).astype(bf16)
 
-    tokens = lax.all_gather(moe_in, "grp", axis=0, tiled=True)
-    outgoing = jnp.dot(
-        select, lax.dynamic_slice_in_dim(tokens, own_at, half, 1), preferred_element_type=f32
-    ).astype(bf16)
+    outgoing = jnp.dot(select, half_gather(moe_in), preferred_element_type=f32).astype(bf16)
     received = lax.all_to_all(
         outgoing.reshape(n_columns, per_source, half), "ep", split_axis=0, concat_axis=0, tiled=True
     ).reshape(-1, half)

time: 383 us -> 314 us (0.82)
  waiting for transfers between devices: 244 us -> 88.8 us
  Pallas kernels: 4.42 us -> 108 us
  blocking collectives: 68.7 us -> 54.3 us
  between operations: 14.7 us -> 1.61 us
  starting transfers between devices: 26.5 us -> 33.2 us
    all_gather x3 -> x0, waiting for transfers between devices: 140 us -> none  [the longest x1 58 us: per_device(): lax.all_gather(caches.reshape(cache_rows, -1), 'ep', axis=0, tiled=True)]
    pallas_call x0 -> x3, Pallas kernels: none -> 103 us  [the longest x1 56.8 us: column_gather(): pl.pallas_call(functools.partial(column_gather_body, columns), out_shape=...]
    ppermute x1, waiting for transfers between devices: 22.2 us -> 0.01 us  [per_device(): w_down = lax.ppermute(w_down, ('grp', 'ep'), trades)]
    all_to_all x1 -> x0, blocking collectives: 12 us -> none  [per_device(): lax.all_to_all(projected, 'grp', split_axis=0, concat_axis=1, tiled=True)]
    all_to_all x0 -> x1, waiting for transfers between devices: none -> 7.4 us  [per_device(): lax.all_to_all(projected, 'grp', split_axis=0, concat_axis=1, tiled=True)]
    all_to_all x0 -> x1, starting transfers between devices: none -> 5.94 us  [per_device(): lax.all_to_all(projected, 'grp', split_axis=0, concat_axis=1, tiled=True)]
  transfers between devices with their start and end apart: 9 -> 7, of which waited for: 8 -> 5; matrix products, arithmetic and copies ran while one was open for 2% -> 3% of each run, Pallas kernels for 0% -> 18%
where the time goes in v3:
time: 314 us; the launch traced here: 313 us
  Pallas kernels  108 us (34%)
  waiting for transfers between devices  88.8 us (28%)
  blocking collectives  54.3 us (17%)
  starting transfers between devices  33.2 us (11%)
  matrix products  18.3 us (6%)
  local copies, waits for them, and re-layouts  5.05 us (2%)
    pallas_call x1, Pallas kernels, column_gather(): pl.pallas_call(functools.partial(column_gather_body, columns), out_shape=...  56.8 us
    all_to_all x1, blocking collectives, per_device(): lax.all_to_all(outgoing.reshape(n_columns, per_source, half), 'ep', split...  54.3 us
    all_to_all x1, waiting for transfers between devices, per_device(): lax.all_to_all(partial_out.reshape(n_columns, per_source, half), 'ep', sp...  48.8 us
    pallas_call x2, Pallas kernels, over_groups(): pl.pallas_call(body, out_shape=jax.ShapeDtypeStruct((n_groups, rows.shape...  46.2 us
    all_to_all x1, waiting for transfers between devices, per_device(): lax.all_to_all(summed.reshape(n_groups, cores * group_slots, half), 'grp'...  27.8 us
    ppermute x1, starting transfers between devices, per_device(): partner = lax.ppermute(received, 'grp', swap)  7.52 us
    all_to_all x1, waiting for transfers between devices, per_device(): lax.all_to_all(projected, 'grp', split_axis=0, concat_axis=1, tiled=True)  7.4 us
  transfers between devices with their start and end apart: 7, of which 5 were waited for; matrix products, arithmetic and copies ran while one was open for 3% of the time, Pallas kernels for 18%

profile of v3, /device:TPU:1, one launch (start us, length us, event | category | flops | bytes accessed | tf_op | source)
XLA Modules:
  0.0 312.6 jit_solution(13738695809695041788)
XLA Ops:
  0.0 4.7 %collective-permute-start = (bf16[2,2048,192]{1,2,0:T(8,128)(2,1)}, bf16[2,2048,192]{1,2,0:T(8,128)(2,1)S(1)}, u32[]{:S(2)}, u32[]{:S(2)}) collective-permute-start(bf16[2,2048,192]{1,2,0:T(8,128)(2,1)} %param.28), channel_id=1, source_target_pairs={{0,0},{1,32},{2,2},{3,34},{4,4},{5,36},{6,6},{7,38},{8,8},{9,40},{... | collective-permute-start | bytes 4718600 | tf_op jit(solution)/shard_map/ppermute | solution.py:325
  4.7 1.9 collective-permute-start.1
  7.3 0.8 copy.37
  8.9 1.6 reshape.173.in_ref
  11.8 56.8 %shard_map.145 = bf16[32,32,2048]{2,1,0:T(8,128)(2,1)} custom-call(bf16[32,2048]{1,0:T(8,128)(2,1)} %reshape.173.in_ref), custom_call_target="tpu_custom_call" | custom-call | flops 1000000000 | bytes 134217728 | tf_op jit(solution)/shard_map/pallas_call | solution.py:115
  68.7 0.7 pad_maximum_fusion
  69.4 5.3 %shard_map.146.in_ref = bf16[16,4224]{1,0:T(8,128)(2,1)} custom-call(s32[1,1]{1,0:T(1,128)} %copy.47.len_ref, s32[1,1]{1,0:T(1,128)S(6)} %copy.48.own_ref, bf16[16,4096]{1,0:T(8,128)(2,1)} %q_ref.1, bf16[16,512]{1,0:T(8,128)(2,1)} %k_ref.1, bf16[16,512]{1,0:T(8,128)(2,1)} %v_ref.1, f32[1,128]{1,0:T(1,128)} %bitcast.71, f32[1,128]{1,0:T(1,128)} %bitcast.72, ...), custom_call_target="tpu_custom_call" | custom-call | tf_op jit(solution)/shard_map/pallas_call | solution.py:277
  74.7 30.5 %shard_map.147 = bf16[16,16,4224]{2,1,0:T(8,128)(2,1)} custom-call(bf16[16,4224]{1,0:T(8,128)(2,1)} %shard_map.146.in_ref), custom_call_target="tpu_custom_call" | custom-call | tf_op jit(solution)/shard_map/pallas_call | solution.py:195
  105.2 0.8 slice.33
  106.5 3.0 fusion.6
  109.5 5.9 %all-to-all-start = ((bf16[16,16,128]{2,1,0:T(8,128)(2,1)}), bf16[16,16,128]{2,1,0:T(8,128)(2,1)S(1)}, u32[]{:S(2)}, u32[]{:S(2)}) async-start(bf16[16,16,128]{2,1,0:T(8,128)(2,1)} %bitcast.5), calls=%async_computation | async-start | bytes 131072 | tf_op jit(solution)/shard_map/all_to_all | solution.py:353
  115.8 7.4 %all-to-all-done = bf16[16,16,128]{2,1,0:T(8,128)(2,1)S(1)} async-done(((bf16[16,16,128]{2,1,0:T(8,128)(2,1)}), bf16[16,16,128]{2,1,0:T(8,128)(2,1)S(1)}, u32[]{:S(2)}, u32[]{:S(2)}) %all-to-all-start) | async-done | bytes 65568 | tf_op jit(solution)/shard_map/all_to_all | solution.py:353
  123.3 0.7 fusion.17.in_ref
  124.1 15.7 %shard_map.148 = bf16[16,16,1024]{2,1,0:T(8,128)(2,1)} custom-call(bf16[16,2048]{1,0:T(8,128)(2,1)} %fusion.17.in_ref), custom_call_target="tpu_custom_call" | custom-call | tf_op jit(solution)/shard_map/pallas_call | solution.py:195
  139.8 1.8 convolution_convert_fusion.1
  141.6 54.3 %all_to_all.28 = bf16[32,32,1024]{2,1,0:T(8,128)(2,1)S(1)} all-to-all(bf16[32,32,1024]{2,1,0:T(8,128)(2,1)S(1)} %bitcast.61), channel_id=1, replica_groups=mesh['grp'=16,'ep'=32] {'ep'}, dimensions={0} | all-to-all | bytes 4194304 | tf_op jit(solution)/shard_map/all_to_all | solution.py:367
  195.9 7.5 %collective-permute-start.2 = (bf16[1024,1024]{1,0:T(8,128)(2,1)S(1)}, bf16[1024,1024]{1,0:T(8,128)(2,1)}, u32[]{:S(2)}, u32[]{:S(2)}) collective-permute-start(bf16[1024,1024]{1,0:T(8,128)(2,1)S(1)} %bitcast.57), channel_id=1, source_target_pairs={{0,32},{32,0},{64,96},{96,64},{128,160},{160,128},{192,224},{224,1... | collective-permute-start | bytes 6291464 | tf_op jit(solution)/shard_map/ppermute | solution.py:370
  203.4 2.0 fusion.12
  205.4 0.8 fusion.11
  206.2 1.0 collective-permute-done.2
  207.3 2.4 convolution_add_fusion.1
  209.7 2.6 fusion.5
  212.4 0.7 convolution_convert_fusion
  213.1 2.3 collective-permute-start.3
  215.4 3.8 %collective-permute-done.3 = bf16[1024,1024]{1,0:T(8,128)(2,1)S(1)} collective-permute-done((bf16[1024,1024]{1,0:T(8,128)(2,1)S(1)}, bf16[1024,1024]{1,0:T(8,128)(2,1)S(1)}, u32[]{:S(2)}, u32[]{:S(2)}) %collective-permute-start.3) | collective-permute-done | bytes 2097184 | tf_op jit(solution)/shard_map/ppermute | solution.py:379
  219.2 2.1 add_convert_fusion
  221.3 4.8 %all-to-all-start.2 = ((bf16[32,32,1024]{2,1,0:T(8,128)(2,1)}), bf16[32,32,1024]{2,1,0:T(8,128)(2,1)S(1)}, u32[]{:S(2)}, u32[]{:S(2)}) async-start(bf16[32,32,1024]{2,1,0:T(8,128)(2,1)} %bitcast.16), calls=%async_computation.2 | async-start | bytes 4194304 | tf_op jit(solution)/shard_map/all_to_all | solution.py:382
  226.1 48.8 %all-to-all-done.2 = bf16[32,32,1024]{2,1,0:T(8,128)(2,1)S(1)} async-done(((bf16[32,32,1024]{2,1,0:T(8,128)(2,1)}), bf16[32,32,1024]{2,1,0:T(8,128)(2,1)S(1)}, u32[]{:S(2)}, u32[]{:S(2)}) %all-to-all-start.2) | async-done | bytes 2097184 | tf_op jit(solution)/shard_map/all_to_all | solution.py:382
  274.9 2.2 fusion.3
  277.1 6.0 %all-to-all-start.3 = ((bf16[16,32,1024]{2,1,0:T(8,128)(2,1)}), bf16[16,32,1024]{2,1,0:T(8,128)(2,1)S(1)}, u32[]{:S(2)}, u32[]{:S(2)}) async-start(bf16[16,32,1024]{2,1,0:T(8,128)(2,1)} %bitcast.69), calls=%async_computation.3 | async-start | bytes 2097152 | tf_op jit(solution)/shard_map/all_to_all | solution.py:396
  283.4 27.8 %all-to-all-done.3 = bf16[16,32,1024]{2,1,0:T(8,128)(2,1)S(1)} async-done(((bf16[16,32,1024]{2,1,0:T(8,128)(2,1)}), bf16[16,32,1024]{2,1,0:T(8,128)(2,1)S(1)}, u32[]{:S(2)}, u32[]{:S(2)}) %all-to-all-start.3) | async-done | bytes 1048608 | tf_op jit(solution)/shard_map/all_to_all | solution.py:396
  311.9 0.7 fusion.19
  (51 shorter events, 3.5 us)
Async XLA Ops:
  0.0 106.5 %copy-start = (bf16[4096,128]{1,0:T(8,128)(2,1)S(1)}, bf16[4096,128]{1,0:T(8,128)(2,1)}, u32[]{:S(2)}) copy-start(bf16[4096,128]{1,0:T(8,128)(2,1)} %param.23) | copy-start | bytes 3145732
  0.0 69.4 %collective-permute-start = (bf16[2,2048,192]{1,2,0:T(8,128)(2,1)}, bf16[2,2048,192]{1,2,0:T(8,128)(2,1)S(1)}, u32[]{:S(2)}, u32[]{:S(2)}) collective-permute-start(bf16[2,2048,192]{1,2,0:T(8,128)(2,1)} %param.28), channel_id=1, source_target_pairs={{0,0},{1,32},{2,2},{3,34},{4,4},{5,36},{6,6},{7,38},{8,8},{9,40},{... | collective-permute-start | bytes 4718600 | tf_op jit(solution)/shard_map/ppermute | solution.py:325
  4.7 64.7 %collective-permute-start.1 = (bf16[192,2048]{1,0:T(8,128)(2,1)}, bf16[192,2048]{1,0:T(8,128)(2,1)S(1)}, u32[]{:S(2)}, u32[]{:S(2)}) collective-permute-start(bf16[192,2048]{1,0:T(8,128)(2,1)} %param.29), channel_id=1, source_target_pairs={{0,0},{1,32},{2,2},{3,34},{4,4},{5,36},{6,6},{7,38},{8,8},{9,40},{... | collective-permute-start | bytes 2359304 | tf_op jit(solution)/shard_map/ppermute | solution.py:326
  69.4 5.3 %copy-start.3 = (bf16[192,2048]{1,0:T(8,128)(2,1)}, bf16[192,2048]{1,0:T(8,128)(2,1)S(1)}, u32[]{:S(2)}) copy-start(bf16[192,2048]{1,0:T(8,128)(2,1)S(1)} %collective-permute-done.1) | copy-start | bytes 2359300
  69.4 5.3 %copy-start.1 = (bf16[2,2048,192]{1,2,0:T(8,128)(2,1)}, bf16[2,2048,192]{1,2,0:T(8,128)(2,1)S(1)}, u32[]{:S(2)}) copy-start(bf16[2,2048,192]{1,2,0:T(8,128)(2,1)S(1)} %collective-permute-done) | copy-start | bytes 4718596
  106.5 16.7 %copy-start.5 = (bf16[16,2048]{1,0:T(8,128)(2,1)S(1)}, bf16[16,2048]{1,0:T(8,128)(2,1)}, u32[]{:S(2)}) copy-start(bf16[16,2048]{1,0:T(8,128)(2,1)} %param.24) | copy-start | bytes 196612
  106.5 16.8 %copy-start.6 = (f32[2048]{0:T(1024)S(1)}, f32[2048]{0:T(1024)}, u32[]{:S(2)}) copy-start(f32[2048]{0:T(1024)} %param.25) | copy-start | bytes 24580
  109.5 13.7 %all-to-all-start = ((bf16[16,16,128]{2,1,0:T(8,128)(2,1)}), bf16[16,16,128]{2,1,0:T(8,128)(2,1)S(1)}, u32[]{:S(2)}, u32[]{:S(2)}) async-start(bf16[16,16,128]{2,1,0:T(8,128)(2,1)} %bitcast.5), calls=%async_computation | async-start | bytes 131072 | tf_op jit(solution)/shard_map/all_to_all | solution.py:353
  195.9 11.4 %collective-permute-start.2 = (bf16[1024,1024]{1,0:T(8,128)(2,1)S(1)}, bf16[1024,1024]{1,0:T(8,128)(2,1)}, u32[]{:S(2)}, u32[]{:S(2)}) collective-permute-start(bf16[1024,1024]{1,0:T(8,128)(2,1)S(1)} %bitcast.57), channel_id=1, source_target_pairs={{0,32},{32,0},{64,96},{96,64},{128,160},{160,128},{192,224},{224,1... | collective-permute-start | bytes 6291464 | tf_op jit(solution)/shard_map/ppermute | solution.py:370
  203.4 2.0 copy-start.2
  209.7 2.6 copy-start.4
  213.1 6.1 %collective-permute-start.3 = (bf16[1024,1024]{1,0:T(8,128)(2,1)S(1)}, bf16[1024,1024]{1,0:T(8,128)(2,1)S(1)}, u32[]{:S(2)}, u32[]{:S(2)}) collective-permute-start(bf16[1024,1024]{1,0:T(8,128)(2,1)S(1)} %convolution_convert_fusion), channel_id=1, source_target_pairs={{0,32},{32,0},{64,96},{96,64},{128,160},{160,128},{192,224},{224,1... | collective-permute-start | bytes 6291464 | tf_op jit(solution)/shard_map/ppermute | solution.py:379
  221.3 53.6 %all-to-all-start.2 = ((bf16[32,32,1024]{2,1,0:T(8,128)(2,1)}), bf16[32,32,1024]{2,1,0:T(8,128)(2,1)S(1)}, u32[]{:S(2)}, u32[]{:S(2)}) async-start(bf16[32,32,1024]{2,1,0:T(8,128)(2,1)} %bitcast.16), calls=%async_computation.2 | async-start | bytes 4194304 | tf_op jit(solution)/shard_map/all_to_all | solution.py:382
  277.1 6.0 %copy-start.7 = (f32[16,8]{0,1:T(8,128)S(1)}, f32[16,8]{0,1:T(8,128)}, u32[]{:S(2)}) copy-start(f32[16,8]{0,1:T(8,128)} %param.27) | copy-start | bytes 1540
  277.1 34.0 %all-to-all-start.3 = ((bf16[16,32,1024]{2,1,0:T(8,128)(2,1)}), bf16[16,32,1024]{2,1,0:T(8,128)(2,1)S(1)}, u32[]{:S(2)}, u32[]{:S(2)}) async-start(bf16[16,32,1024]{2,1,0:T(8,128)(2,1)} %bitcast.69), calls=%async_computation.3 | async-start | bytes 2097152 | tf_op jit(solution)/shard_map/all_to_all | solution.py:396

commit v4 on v3

--- a/solution.py
+++ b/solution.py
@@ -146,18 +146,23 @@
     local.start()
     coming, handed = {}, []
     order = ring_order(depth)
+    lanes = 128
+    width = in_ref.shape[1]
+    middle = width // lanes // 2 * lanes
+    chunks = [pl.ds(0, middle), pl.ds(middle, width - middle)]
     for along in order:
-        here = out_ref.at[(z + along + depth) % depth * 2 + core]
-        if along == 0:
-            source = in_ref
-        else:
-            coming[along].wait_recv()
-            source = here
-        if along <= 0 and along - 1 in order:
-            coming[along - 1] = flights.send(source, here, up)
-        if along >= 0 and along + 1 in order:
-            coming[along + 1] = flights.send(source, here, down)
-        handed.append(flights.send(source, here, partner))
+        for c, chunk in enumerate(chunks):
+            here = out_ref.at[(z + along + depth) % depth * 2 + core, :, chunk]
+            if along == 0:
+                source = in_ref.at[:, chunk]
+            else:
+                coming[along, c].wait_recv()
+                source = here
+            if along <= 0 and along - 1 in order:
+                coming[along - 1, c] = flights.send(source, here, up)
+            if along >= 0 and along + 1 in order:
+                coming[along + 1, c] = flights.send(source, here, down)
+            handed.append(flights.send(source, here, partner))
     for copy in handed:
         copy.wait_recv()
     local.wait()
@@ -208,11 +213,51 @@
 
 
 def group_gather(rows):
-    return over_groups(group_gather_body, lax.axis_size("grp") - 1, rows.shape[1], 1, rows)
+    return over_groups(group_gather_body, 2 * (lax.axis_size("grp") - 1), rows.shape[1], 1, rows)
 
 
 def half_gather(rows):
     return over_groups(half_gather_body, lax.axis_size("grp") // 2, rows.shape[1] // 2, 2, rows)
+
+
+def exchange_body(axis, inner, in_ref, out_ref, local_sem, send_sems, recv_sems):
+    g, p = lax.axis_index("grp"), lax.axis_index("ep")
+    me = lax.axis_index(axis)
+    outer = lax.axis_size(axis) // inner
+    far = lambda n: sorted(range(n), key=lambda d: (-min(d, n - d), d))
+    steps = [(a, b) for b in far(inner) for a in far(outer) if (a, b) != (0, 0)]
+
+    def place(a, b):
+        return (me // inner + a) % outer * inner + (me % inner + b) % inner
+
+    peers = [place(a, b) for a, b in steps]
+    device = (lambda i: (i, p)) if axis == "grp" else (lambda i: (g, i))
+    greet([device(i) for i in peers])
+    flights = Flights(send_sems, recv_sems)
+    copies = [flights.send(in_ref.at[i], out_ref.at[me], device(i)) for i in peers]
+    local = pltpu.make_async_copy(in_ref.at[me], out_ref.at[me], local_sem)
+    local.start()
+    for copy in copies:
+        copy.wait_recv()
+    local.wait()
+    flights.finish()
+
+
+def exchange(blocks, axis, inner, collective_id):
+    count = blocks.shape[0] - 1
+    vmem = pl.BlockSpec(memory_space=pltpu.VMEM)
+    return pl.pallas_call(
+        functools.partial(exchange_body, axis, inner),
+        out_shape=jax.ShapeDtypeStruct(blocks.shape, blocks.dtype),
+        in_specs=[vmem],
+        out_specs=vmem,
+        scratch_shapes=[
+            pltpu.SemaphoreType.DMA,
+            pltpu.SemaphoreType.DMA((count,)),
+            pltpu.SemaphoreType.DMA((count,)),
+        ],
+        compiler_params=pltpu.CompilerParams(collective_id=collective_id, has_side_effects=True),
+    )(blocks)
 
 
 def attention_body(
@@ -350,7 +395,8 @@
     attended = attention(q_raw, k_raw, v_raw, q_gain, k_gain, kv_block, tag, lengths, cont_owner, cache_rows)
     gathered = group_gather(attended)
     projected = jnp.dot(gathered[:, :heads_width], out_weight, preferred_element_type=f32).astype(bf16)
-    attn_proj = lax.all_to_all(projected, "grp", split_axis=0, concat_axis=1, tiled=True)
+    attn_proj = exchange(projected.reshape(n_groups, tok_count, -1), "grp", cores, 3)
+    attn_proj = attn_proj.transpose(1, 0, 2).reshape(tok_count, model_width)
     hidden_state = (residual.astype(f32) + attn_proj.astype(f32)).astype(bf16)
     moe_in = normed(hidden_state.astype(f32), moe_gain).astype(bf16)
 
@@ -364,9 +410,7 @@
     select = (wanted[:, None] == jnp.arange(n_groups * tok_count, dtype=jnp.int32)[None, :]).astype(bf16)
 
     outgoing = jnp.dot(select, half_gather(moe_in), preferred_element_type=f32).astype(bf16)
-    received = lax.all_to_all(
-        outgoing.reshape(n_columns, per_source, half), "ep", split_axis=0, concat_axis=0, tiled=True
-    ).reshape(-1, half)
+    received = exchange(outgoing.reshape(n_columns, per_source, half), "ep", ring_columns, 4).reshape(-1, half)
     partner = lax.ppermute(received, "grp", swap)
 
     def project(which):
@@ -379,9 +423,7 @@
     from_partner = lax.ppermute(for_partner, "grp", swap)
     partial_out = jnp.dot(inner_act, w_down_own, preferred_element_type=f32)
     partial_out = (partial_out + from_partner.astype(f32)).astype(bf16)
-    returned = lax.all_to_all(
-        partial_out.reshape(n_columns, per_source, half), "ep", split_axis=0, concat_axis=0, tiled=True
-    ).reshape(-1, half)
+    returned = exchange(partial_out.reshape(n_columns, per_source, half), "ep", ring_columns, 4).reshape(-1, half)
     in_row = jnp.arange(n_columns * per_source, dtype=jnp.int32)
     in_slot, in_column = in_row % per_source, in_row // per_source
     target = (
@@ -393,9 +435,7 @@
     out_row = jnp.arange(n_groups * cores * group_slots, dtype=jnp.int32)
     gather_sum = (out_row[:, None] == target[None, :]).astype(bf16)
     summed = jnp.dot(gather_sum, returned, preferred_element_type=f32).astype(bf16)
-    expert_out = lax.all_to_all(
-        summed.reshape(n_groups, cores * group_slots, half), "grp", split_axis=0, concat_axis=0, tiled=True
-    )
+    expert_out = exchange(summed.reshape(n_groups, cores * group_slots, half), "grp", cores, 5)
     expert_out = expert_out.reshape(n_groups // cores, cores, cores * group_slots, half).astype(f32)
     moe_out = jnp.concatenate(
         [

time: 314 us -> 311 us (level)
  Pallas kernels: 108 us -> 260 us
  waiting for transfers between devices: 88.8 us -> 1.94 us
  blocking collectives: 54.3 us -> 0 us
  starting transfers between devices: 33.2 us -> 11.5 us
  other arithmetic: 3.11 us -> 6.52 us
    pallas_call x0 -> x4, Pallas kernels: none -> 154 us  [exchange(): pl.pallas_call(functools.partial(exchange_body, axis, inner), out_shape=j...]
    all_to_all x3 -> x0, waiting for transfers between devices: 84 us -> none  [the longest x1 48.8 us: per_device(): lax.all_to_all(partial_out.reshape(n_columns, per_source, half), 'ep', sp...]
    all_to_all x1 -> x0, blocking collectives: 54.3 us -> none  [per_device(): lax.all_to_all(outgoing.reshape(n_columns, per_source, half), 'ep', split...]
    all_to_all x3 -> x0, starting transfers between devices: 16.8 us -> none  [the longest x1 6.04 us: per_device(): lax.all_to_all(summed.reshape(n_groups, cores * group_slots, half), 'grp'...]
    ppermute x1, starting transfers between devices: 7.52 us -> 2.43 us  [per_device(): partner = lax.ppermute(received, 'grp', swap)]
    dot_general x2, matrix products: 5.04 us -> 1.8 us  [project(): jnp.dot(partner, w_in_other[which], preferred_element_type=f32)]
  transfers between devices with their start and end apart: 7 -> 4, of which waited for: 5 -> 2; matrix products, arithmetic and copies ran while one was open for 3% -> 4% of each run, Pallas kernels for 18% -> 18%
where the time goes in v4:
time: 311 us; the launch traced here: 310 us
  Pallas kernels  260 us (84%)
  matrix products  20.4 us (7%)
  starting transfers between devices  11.5 us (4%)
  local copies, waits for them, and re-layouts  7.81 us (3%)
  other arithmetic  6.52 us (2%)
    pallas_call x4, Pallas kernels, exchange(): pl.pallas_call(functools.partial(exchange_body, axis, inner), out_shape=j...  154 us
    pallas_call x1, Pallas kernels, column_gather(): pl.pallas_call(functools.partial(column_gather_body, columns), out_shape=...  55.5 us
    pallas_call x2, Pallas kernels, over_groups(): pl.pallas_call(body, out_shape=jax.ShapeDtypeStruct((n_groups, rows.shape...  45.1 us
  transfers between devices with their start and end apart: 4, of which 2 were waited for; matrix products, arithmetic and copies ran while one was open for 4% of the time, Pallas kernels for 18%

profile of v4, /device:TPU:1, one launch (start us, length us, event | category | flops | bytes accessed | tf_op | source)
XLA Modules:
  0.0 309.8 jit_solution(7727912713783008454)
XLA Ops:
  0.0 4.7 %collective-permute-start = (bf16[2,2048,192]{1,2,0:T(8,128)(2,1)}, bf16[2,2048,192]{1,2,0:T(8,128)(2,1)S(1)}, u32[]{:S(2)}, u32[]{:S(2)}) collective-permute-start(bf16[2,2048,192]{1,2,0:T(8,128)(2,1)} %param.28), channel_id=1, source_target_pairs={{0,0},{1,32},{2,2},{3,34},{4,4},{5,36},{6,6},{7,38},{8,8},{9,40},{... | collective-permute-start | bytes 4718600 | tf_op jit(solution)/shard_map/ppermute | solution.py:370
  4.7 1.9 collective-permute-start.1
  7.3 0.8 copy.31
  8.5 0.7 add_select_fusion
  9.2 0.8 fusion.21
  10.2 1.6 reshape.174.in_ref
  13.1 55.5 %shard_map.145 = bf16[32,32,2048]{2,1,0:T(8,128)(2,1)} custom-call(bf16[32,2048]{1,0:T(8,128)(2,1)} %reshape.174.in_ref), custom_call_target="tpu_custom_call" | custom-call | flops 1000000000 | bytes 134217728 | tf_op jit(solution)/shard_map/pallas_call | solution.py:115
  69.4 5.3 %shard_map.146.in_ref = bf16[16,4224]{1,0:T(8,128)(2,1)} custom-call(s32[1,1]{1,0:T(1,128)} %copy.41.len_ref, s32[1,1]{1,0:T(1,128)S(6)} %copy.42.own_ref, bf16[16,4096]{1,0:T(8,128)(2,1)} %q_ref.1, bf16[16,512]{1,0:T(8,128)(2,1)} %k_ref.1, bf16[16,512]{1,0:T(8,128)(2,1)} %v_ref.1, f32[1,128]{1,0:T(1,128)} %bitcast.73, f32[1,128]{1,0:T(1,128)} %bitcast.74, ...), custom_call_target="tpu_custom_call" | custom-call | tf_op jit(solution)/shard_map/pallas_call | solution.py:322
  74.7 27.7 %shard_map.147 = bf16[16,16,4224]{2,1,0:T(8,128)(2,1)} custom-call(bf16[16,4224]{1,0:T(8,128)(2,1)} %shard_map.146.in_ref), custom_call_target="tpu_custom_call" | custom-call | tf_op jit(solution)/shard_map/pallas_call | solution.py:200
  102.4 0.8 slice.33
  104.2 2.9 fusion.6
  107.1 10.3 %shard_map.148 = bf16[16,16,128]{2,1,0:T(8,128)(2,1)} custom-call(bf16[16,16,128]{2,1,0:T(8,128)(2,1)} %bitcast.72), custom_call_target="tpu_custom_call" | custom-call | tf_op jit(solution)/shard_map/pallas_call | solution.py:249
  117.5 1.0 fusion.15
  119.1 0.7 fusion.17.in_ref
  119.8 17.4 %shard_map.149 = bf16[16,16,1024]{2,1,0:T(8,128)(2,1)} custom-call(bf16[16,2048]{1,0:T(8,128)(2,1)} %fusion.17.in_ref), custom_call_target="tpu_custom_call" | custom-call | tf_op jit(solution)/shard_map/pallas_call | solution.py:200
  137.1 3.2 %convolution_convert_fusion.1 = bf16[1024,1024]{1,0:T(8,128)(2,1)} fusion(bf16[256,1024]{1,0:T(8,128)(2,1)} %bitcast.66, s32[1024]{0:T(1024)S(1)} %eq.72), kind=kOutput, calls=%fused_computation.6 | convolution fusion | flops 538181632 | bytes 2625536 | tf_op jit(solution)/shard_map/dot_general | solution.py:412
  140.3 57.2 %shard_map.150 = bf16[32,32,1024]{2,1,0:T(8,128)(2,1)} custom-call(bf16[32,32,1024]{2,1,0:T(8,128)(2,1)} %bitcast.61), custom_call_target="tpu_custom_call" | custom-call | tf_op jit(solution)/shard_map/pallas_call | solution.py:249
  197.5 2.4 collective-permute-start.2
  200.0 2.6 fusion.12
  202.8 0.8 fusion.11
  203.9 0.8 convolution_add_fusion.1
  204.8 1.0 fusion.5
  205.9 0.8 convolution_convert_fusion
  206.7 2.5 collective-permute-start.3
  210.4 0.8 select_reduce_fusion
  211.3 1.6 collective-permute-done.3
  212.9 3.8 %add_convert_fusion = bf16[1024,1024]{1,0:T(8,128)(2,1)} fusion(bf16[1024,1024]{1,0:T(8,128)(2,1)} %collective-permute-done.3, bf16[1024,192]{0,1:T(8,128)(2,1)S(1)} %fusion.5, bf16[192,2048]{1,0:T(8,128)(2,1)} %copy-done.4, s32[]{:T(128)S(6)} %select_n.110), kind=kOutput, calls=%fused_computation | convolution fusion | flops 405798912 | bytes 4980740 | tf_op jit(solution)/shard_map/dot_general | solution.py:424
  216.7 54.6 %shard_map.151 = bf16[32,32,1024]{2,1,0:T(8,128)(2,1)} custom-call(bf16[32,32,1024]{2,1,0:T(8,128)(2,1)} %bitcast.62), custom_call_target="tpu_custom_call" | custom-call | tf_op jit(solution)/shard_map/pallas_call | solution.py:249
  271.3 3.8 %fusion.3 = bf16[512,1024]{1,0:T(8,128)(2,1)} fusion(bf16[1024,1024]{1,0:T(8,128)(2,1)} %bitcast.67, s32[1024]{0:T(1024)S(1)} %copy-done.13), kind=kOutput, calls=%fused_computation.7 | convolution fusion | flops 1074790400 | bytes 3149824 | tf_op jit(solution)/shard_map/dot_general | solution.py:437
  275.1 32.0 %shard_map.152 = bf16[16,32,1024]{2,1,0:T(8,128)(2,1)} custom-call(bf16[16,32,1024]{2,1,0:T(8,128)(2,1)} %bitcast.70), custom_call_target="tpu_custom_call" | custom-call | tf_op jit(solution)/shard_map/pallas_call | solution.py:249
  307.1 1.3 fusion.60
  309.1 0.7 fusion.19
  (60 shorter events, 6.0 us)
Async XLA Ops:
  0.0 104.1 %copy-start = (bf16[4096,128]{1,0:T(8,128)(2,1)S(1)}, bf16[4096,128]{1,0:T(8,128)(2,1)}, u32[]{:S(2)}) copy-start(bf16[4096,128]{1,0:T(8,128)(2,1)} %param.23) | copy-start | bytes 3145732
  0.0 69.4 %collective-permute-start = (bf16[2,2048,192]{1,2,0:T(8,128)(2,1)}, bf16[2,2048,192]{1,2,0:T(8,128)(2,1)S(1)}, u32[]{:S(2)}, u32[]{:S(2)}) collective-permute-start(bf16[2,2048,192]{1,2,0:T(8,128)(2,1)} %param.28), channel_id=1, source_target_pairs={{0,0},{1,32},{2,2},{3,34},{4,4},{5,36},{6,6},{7,38},{8,8},{9,40},{... | collective-permute-start | bytes 4718600 | tf_op jit(solution)/shard_map/ppermute | solution.py:370
  4.7 64.7 %collective-permute-start.1 = (bf16[192,2048]{1,0:T(8,128)(2,1)}, bf16[192,2048]{1,0:T(8,128)(2,1)S(1)}, u32[]{:S(2)}, u32[]{:S(2)}) collective-permute-start(bf16[192,2048]{1,0:T(8,128)(2,1)} %param.29), channel_id=1, source_target_pairs={{0,0},{1,32},{2,2},{3,34},{4,4},{5,36},{6,6},{7,38},{8,8},{9,40},{... | collective-permute-start | bytes 2359304 | tf_op jit(solution)/shard_map/ppermute | solution.py:371
  7.3 61.3 %copy-start.10 = (pred[16]{0:T(512)(128)(4,1)}, pred[16]{0:T(512)(128)(4,1)S(1)}, u32[]{:S(2)}) copy-start(pred[16]{0:T(512)(128)(4,1)S(1)} %iota_compare_fusion.8) | copy-start | bytes 52
  69.4 5.3 %copy-start.4 = (bf16[192,2048]{1,0:T(8,128)(2,1)}, bf16[192,2048]{1,0:T(8,128)(2,1)S(1)}, u32[]{:S(2)}) copy-start(bf16[192,2048]{1,0:T(8,128)(2,1)S(1)} %collective-permute-done.1) | copy-start | bytes 2359300
  69.4 5.3 %copy-start.2 = (bf16[2,2048,192]{1,2,0:T(8,128)(2,1)}, bf16[2,2048,192]{1,2,0:T(8,128)(2,1)S(1)}, u32[]{:S(2)}) copy-start(bf16[2,2048,192]{1,2,0:T(8,128)(2,1)S(1)} %collective-permute-done) | copy-start | bytes 4718596
  104.2 13.3 %copy-start.8 = (bf16[16,2048]{1,0:T(8,128)(2,1)S(1)}, bf16[16,2048]{1,0:T(8,128)(2,1)}, u32[]{:S(2)}) copy-start(bf16[16,2048]{1,0:T(8,128)(2,1)} %param.24) | copy-start | bytes 196612
  104.2 14.9 %copy-start.9 = (f32[2048]{0:T(1024)S(1)}, f32[2048]{0:T(1024)}, u32[]{:S(2)}) copy-start(f32[2048]{0:T(1024)} %param.25) | copy-start | bytes 24580
  118.4 0.6 copy-start.6
  197.5 6.4 %collective-permute-start.2 = (bf16[1024,1024]{1,0:T(8,128)(2,1)}, bf16[1024,1024]{1,0:T(8,128)(2,1)S(1)}, u32[]{:S(2)}, u32[]{:S(2)}) collective-permute-start(bf16[1024,1024]{1,0:T(8,128)(2,1)} %bitcast.57), channel_id=1, source_target_pairs={{0,32},{32,0},{64,96},{96,64},{128,160},{160,128},{192,224},{224,1... | collective-permute-start | bytes 6291464 | tf_op jit(solution)/shard_map/ppermute | solution.py:414
  200.0 2.6 copy-start.1
  200.0 2.8 copy-start.3
  204.8 1.1 copy-start.5
  205.9 3.2 %copy-start.12 = (f32[16,8]{0,1:T(8,128)S(1)}, f32[16,8]{0,1:T(8,128)}, u32[]{:S(2)}) copy-start(f32[16,8]{0,1:T(8,128)} %param.27) | copy-start | bytes 1540
  206.7 6.2 %collective-permute-start.3 = (bf16[1024,1024]{1,0:T(8,128)(2,1)S(1)}, bf16[1024,1024]{1,0:T(8,128)(2,1)}, u32[]{:S(2)}, u32[]{:S(2)}) collective-permute-start(bf16[1024,1024]{1,0:T(8,128)(2,1)S(1)} %convolution_convert_fusion), channel_id=1, source_target_pairs={{0,32},{32,0},{64,96},{96,64},{128,160},{160,128},{192,224},{224,1... | collective-permute-start | bytes 6291464 | tf_op jit(solution)/shard_map/ppermute | solution.py:423
  216.7 54.6 %copy-start.13 = (s32[1024]{0:T(1024)S(1)}, s32[1024]{0:T(1024)}, u32[]{:S(2)}) copy-start(s32[1024]{0:T(1024)} %fusion.33) | copy-start | bytes 12292
  307.1 2.0 copy-start.7
  307.1 2.0 copy-start.11

commit v5 on v4

--- a/solution.py
+++ b/solution.py
@@ -367,8 +367,6 @@
         for p in range(n_columns):
             to = (g - g % 2 + p % 2) * n_columns + p - p % 2 + g % 2
             trades.append((g * n_columns + p, to))
-    w_in = lax.ppermute(w_in, ("grp", "ep"), trades)
-    w_down = lax.ppermute(w_down, ("grp", "ep"), trades)
     swap = [(g, g ^ 1) for g in range(n_groups)]
 
     flat_route = jnp.where(live_rows[:, None], routes, -1).reshape(-1)
@@ -387,11 +385,8 @@
 
     kv_block = column_gather(caches.reshape(cache_rows, -1), ring_columns, n_columns)
     kv_block, w_in, w_down = lax.optimization_barrier((kv_block, w_in, w_down))
-    own_at, other_at = core * half, (1 - core) * half
-    w_in_own = lax.dynamic_slice_in_dim(w_in, own_at, half, 1)
-    w_in_other = lax.dynamic_slice_in_dim(w_in, other_at, half, 1)
-    w_down_own = lax.dynamic_slice_in_dim(w_down, own_at, half, 1)
-    w_down_other = lax.dynamic_slice_in_dim(w_down, other_at, half, 1)
+    w_in = lax.ppermute(w_in, ("grp", "ep"), trades)
+    w_down = lax.ppermute(w_down, ("grp", "ep"), trades)
     attended = attention(q_raw, k_raw, v_raw, q_gain, k_gain, kv_block, tag, lengths, cont_owner, cache_rows)
     gathered = group_gather(attended)
     projected = jnp.dot(gathered[:, :heads_width], out_weight, preferred_element_type=f32).astype(bf16)
@@ -409,6 +404,12 @@
     wanted = jnp.broadcast_to(wanted[:, None], (local, pieces // cores) + wanted.shape[1:]).reshape(-1)
     select = (wanted[:, None] == jnp.arange(n_groups * tok_count, dtype=jnp.int32)[None, :]).astype(bf16)
 
+    moe_in, w_in, w_down = lax.optimization_barrier((moe_in, w_in, w_down))
+    own_at, other_at = core * half, (1 - core) * half
+    w_in_own = lax.dynamic_slice_in_dim(w_in, own_at, half, 1)
+    w_in_other = lax.dynamic_slice_in_dim(w_in, other_at, half, 1)
+    w_down_own = lax.dynamic_slice_in_dim(w_down, own_at, half, 1)
+    w_down_other = lax.dynamic_slice_in_dim(w_down, other_at, half, 1)
     outgoing = jnp.dot(select, half_gather(moe_in), preferred_element_type=f32).astype(bf16)
     received = exchange(outgoing.reshape(n_columns, per_source, half), "ep", ring_columns, 4).reshape(-1, half)
     partner = lax.ppermute(received, "grp", swap)
@@ -435,7 +436,9 @@
     out_row = jnp.arange(n_groups * cores * group_slots, dtype=jnp.int32)
     gather_sum = (out_row[:, None] == target[None, :]).astype(bf16)
     summed = jnp.dot(gather_sum, returned, preferred_element_type=f32).astype(bf16)
-    expert_out = exchange(summed.reshape(n_groups, cores * group_slots, half), "grp", cores, 5)
+    expert_out = lax.all_to_all(
+        summed.reshape(n_groups, cores * group_slots, half), "grp", split_axis=0, concat_axis=0, tiled=True
+    )
     expert_out = expert_out.reshape(n_groups // cores, cores, cores * group_slots, half).astype(f32)
     moe_out = jnp.concatenate(
         [

time: 311 us -> 302 us (0.971)
  Pallas kernels: 260 us -> 221 us
  waiting for transfers between devices: 1.94 us -> 31.7 us
  starting transfers between devices: 11.5 us -> 16.7 us
  local copies, waits for them, and re-layouts: 7.81 us -> 4.58 us
    pallas_call x4 -> x3, Pallas kernels: 154 us -> 121 us  [exchange(): pl.pallas_call(functools.partial(exchange_body, axis, inner), out_shape=j...]
    all_to_all x0 -> x1, waiting for transfers between devices: none -> 27.8 us  [per_device(): lax.all_to_all(summed.reshape(n_groups, cores * group_slots, half), 'grp'...]
    pallas_call x1, Pallas kernels: 55.5 us -> 47.2 us  [column_gather(): pl.pallas_call(functools.partial(column_gather_body, columns), out_shape=...]
    all_to_all x0 -> x1, starting transfers between devices: none -> 4.99 us  [per_device(): lax.all_to_all(summed.reshape(n_groups, cores * group_slots, half), 'grp'...]
    pallas_call x2, Pallas kernels: 45.1 us -> 48.8 us  [over_groups(): pl.pallas_call(body, out_shape=jax.ShapeDtypeStruct((n_groups, rows.shape...]
  transfers between devices with their start and end apart: 4 -> 5, of which waited for: 2 -> 3; matrix products, arithmetic and copies ran while one was open for 4% -> 4% of each run, Pallas kernels for 18% -> 16%
where the time goes in v5:
time: 302 us; the launch traced here: 300 us
  Pallas kernels  221 us (73%)
  waiting for transfers between devices  31.7 us (10%)
  matrix products  20.6 us (7%)
  starting transfers between devices  16.7 us (6%)
  local copies, waits for them, and re-layouts  4.58 us (2%)
  other arithmetic  3.95 us (1%)
    pallas_call x3, Pallas kernels, exchange(): pl.pallas_call(functools.partial(exchange_body, axis, inner), out_shape=j...  121 us
    pallas_call x2, Pallas kernels, over_groups(): pl.pallas_call(body, out_shape=jax.ShapeDtypeStruct((n_groups, rows.shape...  48.8 us
    pallas_call x1, Pallas kernels, column_gather(): pl.pallas_call(functools.partial(column_gather_body, columns), out_shape=...  47.2 us
    all_to_all x1, waiting for transfers between devices, per_device(): lax.all_to_all(summed.reshape(n_groups, cores * group_slots, half), 'grp'...  27.8 us
  transfers between devices with their start and end apart: 5, of which 3 were waited for; matrix products, arithmetic and copies ran while one was open for 4% of the time, Pallas kernels for 16%

profile of v5, /device:TPU:1, one launch (start us, length us, event | category | flops | bytes accessed | tf_op | source)
XLA Modules:
  0.0 300.3 jit_solution(12482392649909462157)
XLA Ops:
  0.0 1.7 reshape.174.in_ref
  1.7 47.2 %shard_map.145 = bf16[32,32,2048]{2,1,0:T(8,128)(2,1)} custom-call(bf16[32,2048]{1,0:T(8,128)(2,1)} %reshape.174.in_ref), custom_call_target="tpu_custom_call" | custom-call | flops 1000000000 | bytes 134217728 | tf_op jit(solution)/shard_map/pallas_call | solution.py:115
  48.9 4.5 %collective-permute-start = (bf16[2,2048,192]{1,2,0:T(8,128)(2,1)}, bf16[2,2048,192]{1,2,0:T(8,128)(2,1)S(1)}, u32[]{:S(2)}, u32[]{:S(2)}) collective-permute-start(bf16[2,2048,192]{1,2,0:T(8,128)(2,1)} %param.28), channel_id=1, source_target_pairs={{0,0},{1,32},{2,2},{3,34},{4,4},{5,36},{6,6},{7,38},{8,8},{9,40},{... | collective-permute-start | bytes 4718600 | tf_op jit(solution)/shard_map/ppermute | solution.py:388
  53.4 1.9 collective-permute-start.1
  57.6 0.6 pad.4.tag_ref
  58.4 0.7 pad_maximum_fusion
  59.0 4.4 %shard_map.146.in_ref = bf16[16,4224]{1,0:T(8,128)(2,1)} custom-call(s32[1,1]{1,0:T(1,128)} %copy.41.len_ref, s32[1,1]{1,0:T(1,128)S(6)} %copy.42.own_ref, bf16[16,4096]{1,0:T(8,128)(2,1)} %q_ref.1, bf16[16,512]{1,0:T(8,128)(2,1)} %k_ref.1, bf16[16,512]{1,0:T(8,128)(2,1)} %v_ref.1, f32[1,128]{1,0:T(1,128)} %bitcast.72, f32[1,128]{1,0:T(1,128)} %bitcast.73, ...), custom_call_target="tpu_custom_call" | custom-call | tf_op jit(solution)/shard_map/pallas_call | solution.py:322
  63.4 32.4 %shard_map.147 = bf16[16,16,4224]{2,1,0:T(8,128)(2,1)} custom-call(bf16[16,4224]{1,0:T(8,128)(2,1)} %shard_map.146.in_ref), custom_call_target="tpu_custom_call" | custom-call | tf_op jit(solution)/shard_map/pallas_call | solution.py:200
  95.8 0.8 slice.33
  97.2 2.9 fusion.6
  100.1 9.9 %shard_map.148 = bf16[16,16,128]{2,1,0:T(8,128)(2,1)} custom-call(bf16[16,16,128]{2,1,0:T(8,128)(2,1)} %bitcast.71), custom_call_target="tpu_custom_call" | custom-call | tf_op jit(solution)/shard_map/pallas_call | solution.py:249
  110.0 1.0 fusion.15
  111.4 0.7 fusion.17.in_ref
  112.1 16.4 %shard_map.149 = bf16[16,16,1024]{2,1,0:T(8,128)(2,1)} custom-call(bf16[16,2048]{1,0:T(8,128)(2,1)} %fusion.17.in_ref), custom_call_target="tpu_custom_call" | custom-call | tf_op jit(solution)/shard_map/pallas_call | solution.py:200
  128.6 3.1 %convolution_convert_fusion.1 = bf16[1024,1024]{1,0:T(8,128)(2,1)} fusion(bf16[256,1024]{1,0:T(8,128)(2,1)} %bitcast.66, s32[1024]{0:T(1024)S(1)} %eq.72), kind=kOutput, calls=%fused_computation.6 | convolution fusion | flops 538181632 | bytes 2625536 | tf_op jit(solution)/shard_map/dot_general | solution.py:413
  131.7 56.4 %shard_map.150 = bf16[32,32,1024]{2,1,0:T(8,128)(2,1)} custom-call(bf16[32,32,1024]{2,1,0:T(8,128)(2,1)} %bitcast.61), custom_call_target="tpu_custom_call" | custom-call | tf_op jit(solution)/shard_map/pallas_call | solution.py:249
  188.1 2.9 collective-permute-start.2
  191.1 2.6 fusion.12
  193.8 0.8 fusion.11
  194.7 0.3 collective-permute-done.2
  195.0 0.8 convolution_add_fusion.1
  195.9 1.0 fusion.5
  196.8 1.7 convolution_convert_fusion
  198.6 2.5 collective-permute-start.3
  201.0 3.6 %collective-permute-done.3 = bf16[1024,1024]{1,0:T(8,128)(2,1)S(1)} collective-permute-done((bf16[1024,1024]{1,0:T(8,128)(2,1)S(1)}, bf16[1024,1024]{1,0:T(8,128)(2,1)S(1)}, u32[]{:S(2)}, u32[]{:S(2)}) %collective-permute-start.3) | collective-permute-done | bytes 2097184 | tf_op jit(solution)/shard_map/ppermute | solution.py:424
  204.6 3.1 %add_convert_fusion = bf16[1024,1024]{1,0:T(8,128)(2,1)} fusion(bf16[1024,1024]{1,0:T(8,128)(2,1)S(1)} %collective-permute-done.3, bf16[1024,192]{0,1:T(8,128)(2,1)S(1)} %fusion.5, bf16[192,2048]{1,0:T(8,128)(2,1)} %collective-permute-done.1, s32[]{:T(128)S(6)} %select_n.110), kind=kOutput, calls=%fused_computation | convolution fusion | flops 405798912 | bytes 4980740 | tf_op jit(solution)/shard_map/dot_general | solution.py:425
  207.7 54.4 %shard_map.151 = bf16[32,32,1024]{2,1,0:T(8,128)(2,1)} custom-call(bf16[32,32,1024]{2,1,0:T(8,128)(2,1)} %bitcast.62), custom_call_target="tpu_custom_call" | custom-call | tf_op jit(solution)/shard_map/pallas_call | solution.py:249
  262.1 3.8 %fusion.3 = bf16[512,1024]{1,0:T(8,128)(2,1)} fusion(bf16[1024,1024]{1,0:T(8,128)(2,1)} %bitcast.67, s32[1024]{0:T(1024)S(1)} %fusion.33), kind=kOutput, calls=%fused_computation.7 | convolution fusion | flops 1074790400 | bytes 3149824 | tf_op jit(solution)/shard_map/dot_general | solution.py:438
  265.9 5.0 %all-to-all-start = ((bf16[16,32,1024]{2,1,0:T(8,128)(2,1)}), bf16[16,32,1024]{2,1,0:T(8,128)(2,1)S(1)}, u32[]{:S(2)}, u32[]{:S(2)}) async-start(bf16[16,32,1024]{2,1,0:T(8,128)(2,1)} %bitcast.18), calls=%async_computation | async-start | bytes 2097152 | tf_op jit(solution)/shard_map/all_to_all | solution.py:439
  271.1 27.8 %all-to-all-done = bf16[16,32,1024]{2,1,0:T(8,128)(2,1)S(1)} async-done(((bf16[16,32,1024]{2,1,0:T(8,128)(2,1)}), bf16[16,32,1024]{2,1,0:T(8,128)(2,1)S(1)}, u32[]{:S(2)}, u32[]{:S(2)}) %all-to-all-start) | async-done | bytes 1048608 | tf_op jit(solution)/shard_map/all_to_all | solution.py:439
  299.3 0.3 fusion.62
  299.6 0.7 fusion.19
  (49 shorter events, 2.6 us)
Async XLA Ops:
  0.0 97.1 %copy-start = (bf16[4096,128]{1,0:T(8,128)(2,1)S(1)}, bf16[4096,128]{1,0:T(8,128)(2,1)}, u32[]{:S(2)}) copy-start(bf16[4096,128]{1,0:T(8,128)(2,1)} %param.23) | copy-start | bytes 3145732
  1.7 54.3 %copy-start.6 = (s32[16,8]{0,1:T(8,128)S(1)}, s32[16,8]{0,1:T(8,128)}, u32[]{:S(2)}) copy-start(s32[16,8]{0,1:T(8,128)} %param.26) | copy-start | bytes 1540
  48.9 63.2 %collective-permute-start = (bf16[2,2048,192]{1,2,0:T(8,128)(2,1)}, bf16[2,2048,192]{1,2,0:T(8,128)(2,1)S(1)}, u32[]{:S(2)}, u32[]{:S(2)}) collective-permute-start(bf16[2,2048,192]{1,2,0:T(8,128)(2,1)} %param.28), channel_id=1, source_target_pairs={{0,0},{1,32},{2,2},{3,34},{4,4},{5,36},{6,6},{7,38},{8,8},{9,40},{... | collective-permute-start | bytes 4718600 | tf_op jit(solution)/shard_map/ppermute | solution.py:388
  53.4 58.7 %collective-permute-start.1 = (bf16[192,2048]{1,0:T(8,128)(2,1)}, bf16[192,2048]{1,0:T(8,128)(2,1)}, u32[]{:S(2)}, u32[]{:S(2)}) collective-permute-start(bf16[192,2048]{1,0:T(8,128)(2,1)} %param.29), channel_id=1, source_target_pairs={{0,0},{1,32},{2,2},{3,34},{4,4},{5,36},{6,6},{7,38},{8,8},{9,40},{... | collective-permute-start | bytes 2359304 | tf_op jit(solution)/shard_map/ppermute | solution.py:389
  97.0 13.0 %copy-start.4 = (bf16[16,2048]{1,0:T(8,128)(2,1)S(1)}, bf16[16,2048]{1,0:T(8,128)(2,1)}, u32[]{:S(2)}) copy-start(bf16[16,2048]{1,0:T(8,128)(2,1)} %param.24) | copy-start | bytes 196612
  97.1 14.2 %copy-start.5 = (f32[2048]{0:T(1024)S(1)}, f32[2048]{0:T(1024)}, u32[]{:S(2)}) copy-start(f32[2048]{0:T(1024)} %param.25) | copy-start | bytes 24580
  112.1 76.0 %copy-start.2 = (bf16[2,2048,192]{1,2,0:T(8,128)(2,1)}, bf16[2,2048,192]{1,2,0:T(8,128)(2,1)S(1)}, u32[]{:S(2)}) copy-start(bf16[2,2048,192]{1,2,0:T(8,128)(2,1)S(1)} %collective-permute-done) | copy-start | bytes 4718596
  188.1 6.9 %collective-permute-start.2 = (bf16[1024,1024]{1,0:T(8,128)(2,1)}, bf16[1024,1024]{1,0:T(8,128)(2,1)S(1)}, u32[]{:S(2)}, u32[]{:S(2)}) collective-permute-start(bf16[1024,1024]{1,0:T(8,128)(2,1)} %bitcast.57), channel_id=1, source_target_pairs={{0,32},{32,0},{64,96},{96,64},{128,160},{160,128},{192,224},{224,1... | collective-permute-start | bytes 6291464 | tf_op jit(solution)/shard_map/ppermute | solution.py:415
  191.0 2.6 copy-start.1
  191.1 2.8 copy-start.3
  198.6 6.1 %collective-permute-start.3 = (bf16[1024,1024]{1,0:T(8,128)(2,1)S(1)}, bf16[1024,1024]{1,0:T(8,128)(2,1)S(1)}, u32[]{:S(2)}, u32[]{:S(2)}) collective-permute-start(bf16[1024,1024]{1,0:T(8,128)(2,1)S(1)} %convolution_convert_fusion), channel_id=1, source_target_pairs={{0,32},{32,0},{64,96},{96,64},{128,160},{160,128},{192,224},{224,1... | collective-permute-start | bytes 6291464 | tf_op jit(solution)/shard_map/ppermute | solution.py:424
  265.9 5.0 %copy-start.7 = (f32[16,8]{0,1:T(8,128)S(1)}, f32[16,8]{0,1:T(8,128)}, u32[]{:S(2)}) copy-start(f32[16,8]{0,1:T(8,128)} %param.27) | copy-start | bytes 1540
  265.9 33.0 %all-to-all-start = ((bf16[16,32,1024]{2,1,0:T(8,128)(2,1)}), bf16[16,32,1024]{2,1,0:T(8,128)(2,1)S(1)}, u32[]{:S(2)}, u32[]{:S(2)}) async-start(bf16[16,32,1024]{2,1,0:T(8,128)(2,1)} %bitcast.18), calls=%async_computation | async-start | bytes 2097152 | tf_op jit(solution)/shard_map/all_to_all | solution.py:439

commit v6 on v5

--- a/solution.py
+++ b/solution.py
@@ -424,7 +424,9 @@
     from_partner = lax.ppermute(for_partner, "grp", swap)
     partial_out = jnp.dot(inner_act, w_down_own, preferred_element_type=f32)
     partial_out = (partial_out + from_partner.astype(f32)).astype(bf16)
-    returned = exchange(partial_out.reshape(n_columns, per_source, half), "ep", ring_columns, 4).reshape(-1, half)
+    returned = lax.all_to_all(
+        partial_out.reshape(n_columns, per_source, half), "ep", split_axis=0, concat_axis=0, tiled=True
+    ).reshape(-1, half)
     in_row = jnp.arange(n_columns * per_source, dtype=jnp.int32)
     in_slot, in_column = in_row % per_source, in_row // per_source
     target = (

time: 302 us -> 300 us (level)
  Pallas kernels: 221 us -> 167 us
  waiting for transfers between devices: 31.7 us -> 80.5 us
  starting transfers between devices: 16.7 us -> 22.4 us
    pallas_call x3 -> x2, Pallas kernels: 121 us -> 66.4 us  [exchange(): pl.pallas_call(functools.partial(exchange_body, axis, inner), out_shape=j...]
    all_to_all x0 -> x1, waiting for transfers between devices: none -> 48.6 us  [per_device(): lax.all_to_all(partial_out.reshape(n_columns, per_source, half), 'ep', sp...]
    all_to_all x0 -> x1, starting transfers between devices: none -> 4.14 us  [per_device(): lax.all_to_all(partial_out.reshape(n_columns, per_source, half), 'ep', sp...]
  transfers between devices with their start and end apart: 5 -> 6, of which waited for: 3 -> 4; matrix products, arithmetic and copies ran while one was open for 4% -> 4% of each run, Pallas kernels for 16% -> 16%
where the time goes in v6:
time: 300 us; the launch traced here: 299 us
  Pallas kernels  167 us (56%)
  waiting for transfers between devices  80.5 us (27%)
  starting transfers between devices  22.4 us (7%)
  matrix products  19.1 us (6%)
  local copies, waits for them, and re-layouts  4.56 us (2%)
  other arithmetic  3.95 us (1%)
    pallas_call x2, Pallas kernels, exchange(): pl.pallas_call(functools.partial(exchange_body, axis, inner), out_shape=j...  66.4 us
    pallas_call x2, Pallas kernels, over_groups(): pl.pallas_call(body, out_shape=jax.ShapeDtypeStruct((n_groups, rows.shape...  48.8 us
    all_to_all x1, waiting for transfers between devices, per_device(): lax.all_to_all(partial_out.reshape(n_columns, per_source, half), 'ep', sp...  48.6 us
    pallas_call x1, Pallas kernels, column_gather(): pl.pallas_call(functools.partial(column_gather_body, columns), out_shape=...  47.2 us
    all_to_all x1, waiting for transfers between devices, per_device(): lax.all_to_all(summed.reshape(n_groups, cores * group_slots, half), 'grp'...  27.8 us
    all_to_all x1, starting transfers between devices, per_device(): lax.all_to_all(summed.reshape(n_groups, cores * group_slots, half), 'grp'...  6.69 us
  transfers between devices with their start and end apart: 6, of which 4 were waited for; matrix products, arithmetic and copies ran while one was open for 4% of the time, Pallas kernels for 16%

profile of v6, /device:TPU:1, one launch (start us, length us, event | category | flops | bytes accessed | tf_op | source)
XLA Modules:
  0.0 298.9 jit_solution(9466824422643946652)
XLA Ops:
  0.0 1.7 reshape.174.in_ref
  1.7 47.2 %shard_map.145 = bf16[32,32,2048]{2,1,0:T(8,128)(2,1)} custom-call(bf16[32,2048]{1,0:T(8,128)(2,1)} %reshape.174.in_ref), custom_call_target="tpu_custom_call" | custom-call | flops 1000000000 | bytes 134217728 | tf_op jit(solution)/shard_map/pallas_call | solution.py:115
  48.9 4.5 %collective-permute-start = (bf16[2,2048,192]{1,2,0:T(8,128)(2,1)}, bf16[2,2048,192]{1,2,0:T(8,128)(2,1)S(1)}, u32[]{:S(2)}, u32[]{:S(2)}) collective-permute-start(bf16[2,2048,192]{1,2,0:T(8,128)(2,1)} %param.28), channel_id=1, source_target_pairs={{0,0},{1,32},{2,2},{3,34},{4,4},{5,36},{6,6},{7,38},{8,8},{9,40},{... | collective-permute-start | bytes 4718600 | tf_op jit(solution)/shard_map/ppermute | solution.py:388
  53.4 1.9 collective-permute-start.1
  57.6 0.6 pad.4.tag_ref
  58.3 0.7 pad_maximum_fusion
  59.0 4.4 %shard_map.146.in_ref = bf16[16,4224]{1,0:T(8,128)(2,1)} custom-call(s32[1,1]{1,0:T(1,128)} %copy.41.len_ref, s32[1,1]{1,0:T(1,128)S(6)} %copy.42.own_ref, bf16[16,4096]{1,0:T(8,128)(2,1)} %q_ref.1, bf16[16,512]{1,0:T(8,128)(2,1)} %k_ref.1, bf16[16,512]{1,0:T(8,128)(2,1)} %v_ref.1, f32[1,128]{1,0:T(1,128)} %bitcast.72, f32[1,128]{1,0:T(1,128)} %bitcast.73, ...), custom_call_target="tpu_custom_call" | custom-call | tf_op jit(solution)/shard_map/pallas_call | solution.py:322
  63.4 32.4 %shard_map.147 = bf16[16,16,4224]{2,1,0:T(8,128)(2,1)} custom-call(bf16[16,4224]{1,0:T(8,128)(2,1)} %shard_map.146.in_ref), custom_call_target="tpu_custom_call" | custom-call | tf_op jit(solution)/shard_map/pallas_call | solution.py:200
  95.8 0.8 slice.33
  97.1 2.9 fusion.6
  100.1 9.9 %shard_map.148 = bf16[16,16,128]{2,1,0:T(8,128)(2,1)} custom-call(bf16[16,16,128]{2,1,0:T(8,128)(2,1)} %bitcast.71), custom_call_target="tpu_custom_call" | custom-call | tf_op jit(solution)/shard_map/pallas_call | solution.py:249
  110.0 1.0 fusion.15
  111.4 0.7 fusion.17.in_ref
  112.1 16.4 %shard_map.149 = bf16[16,16,1024]{2,1,0:T(8,128)(2,1)} custom-call(bf16[16,2048]{1,0:T(8,128)(2,1)} %fusion.17.in_ref), custom_call_target="tpu_custom_call" | custom-call | tf_op jit(solution)/shard_map/pallas_call | solution.py:200
  128.5 3.1 %convolution_convert_fusion.1 = bf16[1024,1024]{1,0:T(8,128)(2,1)} fusion(bf16[256,1024]{1,0:T(8,128)(2,1)} %bitcast.65, s32[1024]{0:T(1024)S(1)} %eq.72), kind=kOutput, calls=%fused_computation.6 | convolution fusion | flops 538181632 | bytes 2625536 | tf_op jit(solution)/shard_map/dot_general | solution.py:413
  131.7 56.5 %shard_map.150 = bf16[32,32,1024]{2,1,0:T(8,128)(2,1)} custom-call(bf16[32,32,1024]{2,1,0:T(8,128)(2,1)} %bitcast.61), custom_call_target="tpu_custom_call" | custom-call | tf_op jit(solution)/shard_map/pallas_call | solution.py:249
  188.2 2.9 collective-permute-start.2
  191.1 2.6 fusion.12
  193.8 0.8 fusion.11
  195.0 0.8 convolution_add_fusion.1
  195.9 1.0 fusion.5
  196.8 1.7 convolution_convert_fusion
  198.6 2.3 collective-permute-start.3
  200.9 3.8 %collective-permute-done.3 = bf16[1024,1024]{1,0:T(8,128)(2,1)S(1)} collective-permute-done((bf16[1024,1024]{1,0:T(8,128)(2,1)S(1)}, bf16[1024,1024]{1,0:T(8,128)(2,1)S(1)}, u32[]{:S(2)}, u32[]{:S(2)}) %collective-permute-start.3) | collective-permute-done | bytes 2097184 | tf_op jit(solution)/shard_map/ppermute | solution.py:424
  204.6 3.1 %add_convert_fusion = bf16[1024,1024]{1,0:T(8,128)(2,1)} fusion(bf16[1024,1024]{1,0:T(8,128)(2,1)S(1)} %collective-permute-done.3, bf16[1024,192]{0,1:T(8,128)(2,1)S(1)} %fusion.5, bf16[192,2048]{1,0:T(8,128)(2,1)} %collective-permute-done.1, s32[]{:T(128)S(6)} %select_n.110), kind=kOutput, calls=%fused_computation | convolution fusion | flops 405798912 | bytes 4980740 | tf_op jit(solution)/shard_map/dot_general | solution.py:425
  207.7 4.1 %all-to-all-start = ((bf16[32,32,1024]{2,1,0:T(8,128)(2,1)}), bf16[32,32,1024]{2,1,0:T(8,128)(2,1)S(1)}, u32[]{:S(2)}, u32[]{:S(2)}) async-start(bf16[32,32,1024]{2,1,0:T(8,128)(2,1)} %bitcast.16), calls=%async_computation | async-start | bytes 4194304 | tf_op jit(solution)/shard_map/all_to_all | solution.py:427
  211.9 48.6 %all-to-all-done = bf16[32,32,1024]{2,1,0:T(8,128)(2,1)S(1)} async-done(((bf16[32,32,1024]{2,1,0:T(8,128)(2,1)}), bf16[32,32,1024]{2,1,0:T(8,128)(2,1)S(1)}, u32[]{:S(2)}, u32[]{:S(2)}) %all-to-all-start) | async-done | bytes 2097184 | tf_op jit(solution)/shard_map/all_to_all | solution.py:427
  260.5 2.2 fusion.3
  262.7 6.7 %all-to-all-start.1 = ((bf16[16,32,1024]{2,1,0:T(8,128)(2,1)}), bf16[16,32,1024]{2,1,0:T(8,128)(2,1)S(1)}, u32[]{:S(2)}, u32[]{:S(2)}) async-start(bf16[16,32,1024]{2,1,0:T(8,128)(2,1)} %bitcast.69), calls=%async_computation.1 | async-start | bytes 2097152 | tf_op jit(solution)/shard_map/all_to_all | solution.py:441
  269.6 27.8 %all-to-all-done.1 = bf16[16,32,1024]{2,1,0:T(8,128)(2,1)S(1)} async-done(((bf16[16,32,1024]{2,1,0:T(8,128)(2,1)}), bf16[16,32,1024]{2,1,0:T(8,128)(2,1)S(1)}, u32[]{:S(2)}, u32[]{:S(2)}) %all-to-all-start.1) | async-done | bytes 1048608 | tf_op jit(solution)/shard_map/all_to_all | solution.py:441
  297.8 0.3 fusion.62
  298.1 0.7 fusion.19
  (50 shorter events, 2.9 us)
Async XLA Ops:
  0.0 97.1 %copy-start = (bf16[4096,128]{1,0:T(8,128)(2,1)S(1)}, bf16[4096,128]{1,0:T(8,128)(2,1)}, u32[]{:S(2)}) copy-start(bf16[4096,128]{1,0:T(8,128)(2,1)} %param.23) | copy-start | bytes 3145732
  1.7 54.3 %copy-start.6 = (s32[16,8]{0,1:T(8,128)S(1)}, s32[16,8]{0,1:T(8,128)}, u32[]{:S(2)}) copy-start(s32[16,8]{0,1:T(8,128)} %param.26) | copy-start | bytes 1540
  48.9 63.2 %collective-permute-start = (bf16[2,2048,192]{1,2,0:T(8,128)(2,1)}, bf16[2,2048,192]{1,2,0:T(8,128)(2,1)S(1)}, u32[]{:S(2)}, u32[]{:S(2)}) collective-permute-start(bf16[2,2048,192]{1,2,0:T(8,128)(2,1)} %param.28), channel_id=1, source_target_pairs={{0,0},{1,32},{2,2},{3,34},{4,4},{5,36},{6,6},{7,38},{8,8},{9,40},{... | collective-permute-start | bytes 4718600 | tf_op jit(solution)/shard_map/ppermute | solution.py:388
  53.4 58.7 %collective-permute-start.1 = (bf16[192,2048]{1,0:T(8,128)(2,1)}, bf16[192,2048]{1,0:T(8,128)(2,1)}, u32[]{:S(2)}, u32[]{:S(2)}) collective-permute-start(bf16[192,2048]{1,0:T(8,128)(2,1)} %param.29), channel_id=1, source_target_pairs={{0,0},{1,32},{2,2},{3,34},{4,4},{5,36},{6,6},{7,38},{8,8},{9,40},{... | collective-permute-start | bytes 2359304 | tf_op jit(solution)/shard_map/ppermute | solution.py:389
  97.0 13.0 %copy-start.4 = (bf16[16,2048]{1,0:T(8,128)(2,1)S(1)}, bf16[16,2048]{1,0:T(8,128)(2,1)}, u32[]{:S(2)}) copy-start(bf16[16,2048]{1,0:T(8,128)(2,1)} %param.24) | copy-start | bytes 196612
  97.1 14.2 %copy-start.5 = (f32[2048]{0:T(1024)S(1)}, f32[2048]{0:T(1024)}, u32[]{:S(2)}) copy-start(f32[2048]{0:T(1024)} %param.25) | copy-start | bytes 24580
  112.1 76.1 %copy-start.2 = (bf16[2,2048,192]{1,2,0:T(8,128)(2,1)}, bf16[2,2048,192]{1,2,0:T(8,128)(2,1)S(1)}, u32[]{:S(2)}) copy-start(bf16[2,2048,192]{1,2,0:T(8,128)(2,1)S(1)} %collective-permute-done) | copy-start | bytes 4718596
  188.2 6.9 %collective-permute-start.2 = (bf16[1024,1024]{1,0:T(8,128)(2,1)}, bf16[1024,1024]{1,0:T(8,128)(2,1)S(1)}, u32[]{:S(2)}, u32[]{:S(2)}) collective-permute-start(bf16[1024,1024]{1,0:T(8,128)(2,1)} %bitcast.57), channel_id=1, source_target_pairs={{0,32},{32,0},{64,96},{96,64},{128,160},{160,128},{192,224},{224,1... | collective-permute-start | bytes 6291464 | tf_op jit(solution)/shard_map/ppermute | solution.py:415
  191.0 2.6 copy-start.1
  191.1 2.8 copy-start.3
  198.6 6.1 %collective-permute-start.3 = (bf16[1024,1024]{1,0:T(8,128)(2,1)S(1)}, bf16[1024,1024]{1,0:T(8,128)(2,1)S(1)}, u32[]{:S(2)}, u32[]{:S(2)}) collective-permute-start(bf16[1024,1024]{1,0:T(8,128)(2,1)S(1)} %convolution_convert_fusion), channel_id=1, source_target_pairs={{0,32},{32,0},{64,96},{96,64},{128,160},{160,128},{192,224},{224,1... | collective-permute-start | bytes 6291464 | tf_op jit(solution)/shard_map/ppermute | solution.py:424
  207.7 52.8 %all-to-all-start = ((bf16[32,32,1024]{2,1,0:T(8,128)(2,1)}), bf16[32,32,1024]{2,1,0:T(8,128)(2,1)S(1)}, u32[]{:S(2)}, u32[]{:S(2)}) async-start(bf16[32,32,1024]{2,1,0:T(8,128)(2,1)} %bitcast.16), calls=%async_computation | async-start | bytes 4194304 | tf_op jit(solution)/shard_map/all_to_all | solution.py:427
  262.7 6.7 %copy-start.7 = (f32[16,8]{0,1:T(8,128)S(1)}, f32[16,8]{0,1:T(8,128)}, u32[]{:S(2)}) copy-start(f32[16,8]{0,1:T(8,128)} %param.27) | copy-start | bytes 1540
  262.7 34.7 %all-to-all-start.1 = ((bf16[16,32,1024]{2,1,0:T(8,128)(2,1)}), bf16[16,32,1024]{2,1,0:T(8,128)(2,1)S(1)}, u32[]{:S(2)}, u32[]{:S(2)}) async-start(bf16[16,32,1024]{2,1,0:T(8,128)(2,1)} %bitcast.69), calls=%async_computation.1 | async-start | bytes 2097152 | tf_op jit(solution)/shard_map/all_to_all | solution.py:441
